TPU v7x, 128 devices: a whole 4x4x4 slice. The times are simulated.
128 devices in a mesh: grp: 8 (over y_lo, z), wide: 16 (over y_hi, x, core).
Axes of the slice: x: 4, y: 4 (y_hi: 2, y_lo: 2; y = y_hi * 2 + y_lo), z: 4, core: 2. Of those that a mesh axis runs over, the one named last changes fastest.
Arguments:
- half_integrals: bfloat16 [16, 8, 1024, 2048], P('wide', None, None, 'grp'), may hold values from -0.47851562 to 0.47851562
- coeff_virtual: bfloat16 [1024, 768], replicated, may hold values from -0.1875 to 0.1875
- occ_energy: float32 [16, 8], replicated, may hold values from -2 to -0.3
- vir_energy: float32 [768], replicated, may hold values from 0.2 to 3
- plan: int32 [2, 2], replicated, may hold values from 0 to 15, as said below
Outputs:
- density_three: float32 [16, 8, 768, 2048], P('wide', 'grp')
Inputs may be any that keep to these rules, and one draw needn't show every extreme that they name: plan[s, k] is the owner block whose orbitals serve step s, slot k; the value 0 and the value 16 - 1 both occur in every draw, an owner may repeat.
All inputs are finite; a program needn't handle non-finite values.
Results may differ from a plain program's by a relative error of at most 0.0039.
Values may be sent and summed in bfloat16 or wider, within the bound.
No kernel may reach another device: no remote copies, remote signals or barrier semaphores. Data moves between devices by JAX's collectives and lax.ppermute only.
A program may use at most 128 MiB of HBM per device.

v0:
```python
import jax
import jax.numpy as jnp
from jax import lax
from jax.experimental import pallas as pl
from jax.experimental.pallas import tpu as pltpu
from jax.sharding import Mesh, PartitionSpec as P


GRP = ("ylo", "z")
WIDE = ("yhi", "x", "core")
ALL = GRP + WIDE
NWIDE = 16
NGRP = 8


def swap(value, axis):
    return lax.ppermute(value, axis, [(0, 1), (1, 0)])


def shift(value, step):
    return lax.ppermute(value, "x", [(i, (i + step) % 4) for i in range(4)])


def gather_wide(own):
    other = swap(own, "yhi")
    own_r = shift(own, 1)
    own_l = shift(own, -1)
    other, own_r, own_l = lax.optimization_barrier((other, own_r, own_l))
    oth_l = shift(other, -1)
    oth_r = shift(other, 1)
    own_far = shift(own_r, 1)
    oth_far = shift(oth_l, -1)
    mine = [own, other, own_r, own_l, oth_r, oth_l, own_far, oth_far]
    return mine + [swap(block, "core") for block in mine]


def pick_kernel(plan_ref, spread_ref, out_ref, sem):
    cols = spread_ref.shape[3]
    copies = []
    for k in range(4):
        owner = plan_ref[k // 2, k % 2]
        for g in range(NGRP):
            copies.append(pltpu.make_async_copy(
                spread_ref.at[g, owner], out_ref.at[k, :, pl.ds(g * cols, cols)], sem))
    for c in copies:
        c.start()
    for c in copies:
        c.wait()


def pick_owners(plan, spread):
    part, cols = spread.shape[2:]
    return pl.pallas_call(
        pick_kernel,
        out_shape=jax.ShapeDtypeStruct((4, part, NGRP * cols), spread.dtype),
        in_specs=[pl.BlockSpec(memory_space=pltpu.SMEM), pl.BlockSpec(memory_space=pl.ANY)],
        out_specs=pl.BlockSpec(memory_space=pltpu.VMEM),
        scratch_shapes=[pltpu.SemaphoreType.DMA],
        name="pick_owners",
    )(plan, spread)


def block_indices():
    yhi, x, core = (lax.axis_index(a) for a in WIDE)
    places = [(0, 0), (1, 0), (0, 3), (0, 1), (1, 3), (1, 1), (0, 2), (1, 2)]
    out = []
    for flip in (0, 1):
        for dy, dx in places:
            out.append(((yhi ^ dy) * 4 + (x + dx) % 4) * 2 + (core ^ flip))
    return jnp.stack(out).astype(jnp.int32)


def pair_kernel(count, *refs):
    where_ref, energy_ref, vir_ref, rows_i_ref = refs[:4]
    blocks = refs[4:4 + NWIDE]
    out_ref, rows_i, rows_j, amp, comb, obuf, in_sem, out_sem = refs[4 + NWIDE:]
    virt, aux = rows_i.shape
    part = blocks[0].shape[1]
    wide_p = rows_i_ref.shape[2]
    step = obuf.shape[2]
    nstep = aux // step
    copies = [[] for _ in range(count)]
    for g in range(NGRP):
        copies[0].append(pltpu.make_async_copy(
            rows_i_ref.at[g], rows_i.at[:, pl.ds(g * wide_p, wide_p)], in_sem.at[0]))
    for k in range(count):
        for b in range(NWIDE):
            start = pl.multiple_of(where_ref[b] * part, 16)
            copies[k].append(pltpu.make_async_copy(
                blocks[b].at[k], rows_j.at[pl.ds(k * virt + start, part), :], in_sem.at[k]))
    for group in copies:
        for c in group:
            c.start()

    def out_copy(n):
        return pltpu.make_async_copy(
            obuf.at[n % 2], out_ref.at[:, pl.ds(n * step, step)], out_sem.at[n % 2])

    vrow = vir_ref[...]
    vcol = jnp.broadcast_to(vrow, (128, virt)).T[:, :1]
    tile = 256
    for k in range(count):
        for c in copies[k]:
            c.wait()
        inter = lax.dot_general(
            rows_i[...], rows_j[k * virt:(k + 1) * virt, :], (((1,), (1,)), ((), ())),
            preferred_element_type=jnp.float32)
        amp[...] = inter / ((energy_ref[0] + energy_ref[1 + k]) - vcol - vrow)
        for i in range(virt // tile):
            for j in range(virt // tile):
                here = amp[i * tile:(i + 1) * tile, j * tile:(j + 1) * tile]
                there = amp[j * tile:(j + 1) * tile, i * tile:(i + 1) * tile]
                comb[i * tile:(i + 1) * tile, k * virt + j * tile:k * virt + (j + 1) * tile] = (
                    2.0 * here - there.T).astype(jnp.bfloat16)
    for n in range(nstep):
        total = jnp.dot(comb[...], rows_j[:, n * step:(n + 1) * step],
                        preferred_element_type=jnp.float32)
        if n >= 2:
            out_copy(n - 2).wait()
        obuf[n % 2] = total
        out_copy(n).start()
    for n in range(max(nstep - 2, 0), nstep):
        out_copy(n).wait()


def pair_terms(where, energies, vir, rows_i, blocks):
    count, _, aux = blocks[0].shape
    virt = rows_i.shape[1]
    step = 512
    anyspec = pl.BlockSpec(memory_space=pl.ANY)
    smem = pl.BlockSpec(memory_space=pltpu.SMEM)
    vmem = pl.BlockSpec(memory_space=pltpu.VMEM)

    def body(*refs):
        pair_kernel(count, *refs)

    return pl.pallas_call(
        body,
        out_shape=jax.ShapeDtypeStruct((virt, aux), jnp.float32),
        in_specs=[smem, smem, vmem] + [anyspec] * (1 + NWIDE),
        out_specs=anyspec,
        scratch_shapes=[
            pltpu.VMEM((virt, aux), jnp.bfloat16),
            pltpu.VMEM((count * virt, aux), jnp.bfloat16),
            pltpu.VMEM((virt, virt), jnp.float32),
            pltpu.VMEM((virt, count * virt), jnp.bfloat16),
            pltpu.VMEM((2, virt, step), jnp.float32),
            pltpu.SemaphoreType.DMA((count,)),
            pltpu.SemaphoreType.DMA((2,)),
        ],
        compiler_params=pltpu.CompilerParams(vmem_limit_bytes=56 * 1024 * 1024),
        cost_estimate=pl.CostEstimate(
            flops=4 * count * virt * virt * aux, transcendentals=0,
            bytes_accessed=2 * (count + 1) * virt * aux + 4 * virt * aux),
        name="pair_terms",
    )(where, energies, vir, rows_i, *blocks)


def shards(half_integrals, coeff_virtual, occ_energy, vir_energy, plan):
    rows = jnp.einsum(
        "imp,ma->iap", half_integrals[0], coeff_virtual, preferred_element_type=jnp.float32
    ).astype(jnp.bfloat16)
    orbs, virt, cols = rows.shape
    part = virt // NWIDE
    spread = lax.all_to_all(rows.reshape(orbs * NWIDE, part, cols), ALL, 0, 0, tiled=True)
    spread = spread.reshape(NGRP, NWIDE, part, cols)
    owners = plan.reshape(-1)
    grp = lax.axis_index(GRP)
    wide = lax.axis_index(WIDE)
    energy = lax.dynamic_slice_in_dim(occ_energy, grp, 1, 1)[:, 0]
    my_energy = lax.dynamic_slice_in_dim(energy, wide, 1)
    e_own = jnp.take(energy, owners, axis=0)
    small = (block_indices(), jnp.concatenate([my_energy, e_own]), vir_energy[None, :])
    spread, (where, energies, vrow) = lax.optimization_barrier((spread, small))
    picked, rows = lax.optimization_barrier((pick_owners(plan, spread), rows))
    blocks = gather_wide(picked)
    rows_i = lax.all_to_all(rows, GRP, 0, 0, tiled=True)
    return pair_terms(where, energies, vrow, rows_i, blocks)[None, None]


def solution(mesh):
    fine = Mesh(mesh.devices.reshape(2, 4, 2, 4, 2), GRP + WIDE)
    return jax.shard_map(
        shards,
        mesh=fine,
        in_specs=(P(WIDE, None, None, GRP), P(), P(), P(), P()),
        out_specs=P(WIDE, GRP, None, None),
        check_vma=False,
    )
```

profile of v0, /device:TPU:0, one launch (start us, length us, event | category | flops | bytes accessed | tf_op | source)
XLA Modules:
  0.0 160.7 jit_solution(7142377228935703221)
XLA Ops:
  0.0 1.4 copy-done
  1.4 7.0 %fusion.2 = bf16[768,8,256]{2,0,1:T(8,128)(2,1)} fusion(bf16[1,8,1024,256]{3,2,1,0:T(8,128)(2,1)} %param.5, bf16[1024,768]{1,0:T(8,128)(2,1)S(1)} %copy-done), kind=kOutput, calls=%fused_computation.3 | convolution fusion | flops 3222798336 | bytes 8912896 | tf_op jit(solution)/shard_map/imp,ma->iap/dot_general | solution.py:160
  8.4 11.6 %all-to-all-start = ((bf16[128,48,256]{2,1,0:T(8,128)(2,1)}), bf16[128,48,256]{2,1,0:T(8,128)(2,1)}, u32[]{:S(2)}, u32[]{:S(2)}) async-start(bf16[128,48,256]{2,1,0:T(8,128)(2,1)} %bitcast.34), calls=%async_computation | async-start | bytes 6291456 | tf_op jit(solution)/shard_map/all_to_all | solution.py:165
  20.9 1.3 dynamic_slice.8
  22.2 0.7 dynamic-slice_bitcast_fusion
  24.2 1.2 pad_maximum_fusion.refs_1_
  25.4 36.0 %all-to-all-done = bf16[128,48,256]{2,1,0:T(8,128)(2,1)} async-done(((bf16[128,48,256]{2,1,0:T(8,128)(2,1)}), bf16[128,48,256]{2,1,0:T(8,128)(2,1)}, u32[]{:S(2)}, u32[]{:S(2)}) %all-to-all-start) | async-done | bytes 3145760 | tf_op jit(solution)/shard_map/all_to_all | solution.py:165
  61.3 2.7 %pick_owners.1.refs_4_ = bf16[4,48,2048]{2,1,0:T(8,128)(2,1)} custom-call(s32[2,2]{1,0:T(2,128)} %plan_ref.1, bf16[8,16,48,256]{3,2,1,0:T(8,128)(2,1)} %bitcast.4.spread_ref), custom_call_target="tpu_custom_call" | custom-call | tf_op jit(solution)/shard_map/pick_owners/pallas_call | solution.py:53
  64.2 1.9 %collective-permute-start.1 = (bf16[4,48,2048]{2,1,0:T(8,128)(2,1)}, bf16[4,48,2048]{2,1,0:T(8,128)(2,1)}, u32[]{:S(2)}, u32[]{:S(2)}) collective-permute-start(bf16[4,48,2048]{2,1,0:T(8,128)(2,1)} %pick_owners.1.refs_4_), channel_id=1, source_target_pairs={{0,2},{2,4},{4,6},{6,0},{1,3},{3,5},{5,7},{7,1},{8,10},{10,12},{12... | collective-permute-start | bytes 2359304 | tf_op jit(solution)/shard_map/ppermute | solution.py:21
  66.4 4.5 %all-to-all-start.1 = ((bf16[8,768,256]{2,1,0:T(8,128)(2,1)}), bf16[8,768,256]{2,1,0:T(8,128)(2,1)}, u32[]{:S(2)}, u32[]{:S(2)}) async-start(bf16[8,768,256]{2,1,0:T(8,128)(2,1)} %bitcast.35), calls=%async_computation.1 | async-start | bytes 6291456 | tf_op jit(solution)/shard_map/all_to_all | solution.py:177
  70.9 0.7 collective-permute-start.7
  71.6 11.4 %collective-permute-done.2.refs_7_ = bf16[4,48,2048]{2,1,0:T(8,128)(2,1)S(1)} collective-permute-done((bf16[4,48,2048]{2,1,0:T(8,128)(2,1)}, bf16[4,48,2048]{2,1,0:T(8,128)(2,1)S(1)}, u32[]{:S(2)}, u32[]{:S(2)}) %collective-permute-start.2) | collective-permute-done | bytes 786464 | tf_op jit(solution)/shard_map/ppermute | solution.py:21
  83.0 2.5 %collective-permute-done.1.refs_6_ = bf16[4,48,2048]{2,1,0:T(8,128)(2,1)} collective-permute-done((bf16[4,48,2048]{2,1,0:T(8,128)(2,1)}, bf16[4,48,2048]{2,1,0:T(8,128)(2,1)}, u32[]{:S(2)}, u32[]{:S(2)}) %collective-permute-start.1) | collective-permute-done | bytes 786464 | tf_op jit(solution)/shard_map/ppermute | solution.py:21
  85.5 2.9 %collective-permute-done.refs_5_ = bf16[4,48,2048]{2,1,0:T(8,128)(2,1)} collective-permute-done((bf16[4,48,2048]{2,1,0:T(8,128)(2,1)}, bf16[4,48,2048]{2,1,0:T(8,128)(2,1)}, u32[]{:S(2)}, u32[]{:S(2)}) %collective-permute-start) | collective-permute-done | bytes 786464 | tf_op jit(solution)/shard_map/ppermute | solution.py:17
  88.3 1.4 collective-permute-start.4
  90.2 0.7 collective-permute-start.5
  91.4 13.7 %collective-permute-done.4.refs_9_ = bf16[4,48,2048]{2,1,0:T(8,128)(2,1)S(1)} collective-permute-done((bf16[4,48,2048]{2,1,0:T(8,128)(2,1)}, bf16[4,48,2048]{2,1,0:T(8,128)(2,1)S(1)}, u32[]{:S(2)}, u32[]{:S(2)}) %collective-permute-start.4) | collective-permute-done | bytes 786464 | tf_op jit(solution)/shard_map/ppermute | solution.py:21
  105.1 3.6 %collective-permute-start.6 = (bf16[4,48,2048]{2,1,0:T(8,128)(2,1)S(1)}, bf16[4,48,2048]{2,1,0:T(8,128)(2,1)}, u32[]{:S(2)}, u32[]{:S(2)}) collective-permute-start(bf16[4,48,2048]{2,1,0:T(8,128)(2,1)S(1)} %collective-permute-done.4.refs_9_), channel_id=1, source_target_pairs={{0,6},{2,0},{4,2},{6,4},{1,7},{3,1},{5,3},{7,5},{8,14},{10,8},{12,... | collective-permute-start | bytes 2359304 | tf_op jit(solution)/shard_map/ppermute | solution.py:21
  109.4 2.7 %collective-permute-done.5.refs_10_ = bf16[4,48,2048]{2,1,0:T(8,128)(2,1)S(1)} collective-permute-done((bf16[4,48,2048]{2,1,0:T(8,128)(2,1)}, bf16[4,48,2048]{2,1,0:T(8,128)(2,1)S(1)}, u32[]{:S(2)}, u32[]{:S(2)}) %collective-permute-start.5) | collective-permute-done | bytes 786464 | tf_op jit(solution)/shard_map/ppermute | solution.py:21
  112.0 15.9 %collective-permute-done.3.refs_8_ = bf16[4,48,2048]{2,1,0:T(8,128)(2,1)S(1)} collective-permute-done((bf16[4,48,2048]{2,1,0:T(8,128)(2,1)}, bf16[4,48,2048]{2,1,0:T(8,128)(2,1)S(1)}, u32[]{:S(2)}, u32[]{:S(2)}) %collective-permute-start.3) | collective-permute-done | bytes 786464 | tf_op jit(solution)/shard_map/ppermute | solution.py:21
  128.5 0.8 copy-done.11
  129.6 0.9 copy-done.12
  130.5 1.0 collective-permute-done.14.refs_19_
  131.5 29.0 %pair_terms.1 = f32[768,2048]{1,0:T(8,128)} custom-call(s32[16]{0:T(128)} %stack.67.refs_0_, f32[5]{0:T(128)} %pad_maximum_fusion.refs_1_, f32[1,768]{1,0:T(1,128)} %broadcast_in_dim.8.refs_2_, bf16[8,768,256]{2,1,0:T(8,128)(2,1)} %all-to-all-done.1.refs_3_, bf16[4,48,2048]{2,1,0:T(8,128)(2,1)} %pick_owners.1.refs_4_, ...), custom_call_target="tpu_custom_call" | custom-call | flops 19327352832 | bytes 22020096 | tf_op jit(solution)/shard_map/pair_terms/pallas_call | solution.py:137
  (52 shorter events, 5.1 us)
Async XLA Ops:
  8.4 11.7 %copy-start.3 = (s32[2,2]{1,0:T(2,128)S(1)}, s32[2,2]{1,0:T(2,128)}, u32[]{:S(2)}) copy-start(s32[2,2]{1,0:T(2,128)} %plan_ref.1) | copy-start | bytes 52
  8.4 11.9 %copy-start.2 = (f32[768]{0:T(1024)S(1)}, f32[768]{0:T(1024)}, u32[]{:S(2)}) copy-start(f32[768]{0:T(1024)} %param.8) | copy-start | bytes 9220
  8.4 52.9 %all-to-all-start = ((bf16[128,48,256]{2,1,0:T(8,128)(2,1)}), bf16[128,48,256]{2,1,0:T(8,128)(2,1)}, u32[]{:S(2)}, u32[]{:S(2)}) async-start(bf16[128,48,256]{2,1,0:T(8,128)(2,1)} %bitcast.34), calls=%async_computation | async-start | bytes 6291456 | tf_op jit(solution)/shard_map/all_to_all | solution.py:165
  64.0 19.0 %collective-permute-start.2 = (bf16[4,48,2048]{2,1,0:T(8,128)(2,1)}, bf16[4,48,2048]{2,1,0:T(8,128)(2,1)S(1)}, u32[]{:S(2)}, u32[]{:S(2)}) collective-permute-start(bf16[4,48,2048]{2,1,0:T(8,128)(2,1)} %pick_owners.1.refs_4_), channel_id=1, source_target_pairs={{0,6},{2,0},{4,2},{6,4},{1,7},{3,1},{5,3},{7,5},{8,14},{10,8},{12,... | collective-permute-start | bytes 2359304 | tf_op jit(solution)/shard_map/ppermute | solution.py:21
  64.2 21.2 %collective-permute-start.1 = (bf16[4,48,2048]{2,1,0:T(8,128)(2,1)}, bf16[4,48,2048]{2,1,0:T(8,128)(2,1)}, u32[]{:S(2)}, u32[]{:S(2)}) collective-permute-start(bf16[4,48,2048]{2,1,0:T(8,128)(2,1)} %pick_owners.1.refs_4_), channel_id=1, source_target_pairs={{0,2},{2,4},{4,6},{6,0},{1,3},{3,5},{5,7},{7,1},{8,10},{10,12},{12... | collective-permute-start | bytes 2359304 | tf_op jit(solution)/shard_map/ppermute | solution.py:21
  66.1 22.2 %collective-permute-start = (bf16[4,48,2048]{2,1,0:T(8,128)(2,1)}, bf16[4,48,2048]{2,1,0:T(8,128)(2,1)}, u32[]{:S(2)}, u32[]{:S(2)}) collective-permute-start(bf16[4,48,2048]{2,1,0:T(8,128)(2,1)} %pick_owners.1.refs_4_), channel_id=1, source_target_pairs={{0,8},{8,0},{1,9},{9,1},{2,10},{10,2},{3,11},{11,3},{4,12},{12,4},... | collective-permute-start | bytes 2359304 | tf_op jit(solution)/shard_map/ppermute | solution.py:17
  66.4 64.1 %all-to-all-start.1 = ((bf16[8,768,256]{2,1,0:T(8,128)(2,1)}), bf16[8,768,256]{2,1,0:T(8,128)(2,1)}, u32[]{:S(2)}, u32[]{:S(2)}) async-start(bf16[8,768,256]{2,1,0:T(8,128)(2,1)} %bitcast.35), calls=%async_computation.1 | async-start | bytes 6291456 | tf_op jit(solution)/shard_map/all_to_all | solution.py:177
  70.9 20.0 %collective-permute-start.7 = (bf16[4,48,2048]{2,1,0:T(8,128)(2,1)S(1)}, bf16[4,48,2048]{2,1,0:T(8,128)(2,1)S(1)}, u32[]{:S(2)}, u32[]{:S(2)}) collective-permute-start(bf16[4,48,2048]{2,1,0:T(8,128)(2,1)S(1)} %copy-done.1), channel_id=1, source_target_pairs={{0,1},{1,0},{2,3},{3,2},{4,5},{5,4},{6,7},{7,6},{8,9},{9,8},{10,11... | collective-permute-start | bytes 2359304 | tf_op jit(solution)/shard_map/ppermute | solution.py:17
  83.0 48.5 %copy-start.4 = (bf16[4,48,2048]{2,1,0:T(8,128)(2,1)}, bf16[4,48,2048]{2,1,0:T(8,128)(2,1)S(1)}, u32[]{:S(2)}) copy-start(bf16[4,48,2048]{2,1,0:T(8,128)(2,1)S(1)} %collective-permute-done.2.refs_7_) | copy-start | bytes 2359300
  88.3 16.8 %collective-permute-start.4 = (bf16[4,48,2048]{2,1,0:T(8,128)(2,1)}, bf16[4,48,2048]{2,1,0:T(8,128)(2,1)S(1)}, u32[]{:S(2)}, u32[]{:S(2)}) collective-permute-start(bf16[4,48,2048]{2,1,0:T(8,128)(2,1)} %collective-permute-done.refs_5_), channel_id=1, source_target_pairs={{0,6},{2,0},{4,2},{6,4},{1,7},{3,1},{5,3},{7,5},{8,14},{10,8},{12,... | collective-permute-start | bytes 2359304 | tf_op jit(solution)/shard_map/ppermute | solution.py:21
  89.7 19.0 %collective-permute-start.10 = (bf16[4,48,2048]{2,1,0:T(8,128)(2,1)S(1)}, bf16[4,48,2048]{2,1,0:T(8,128)(2,1)S(1)}, u32[]{:S(2)}, u32[]{:S(2)}) collective-permute-start(bf16[4,48,2048]{2,1,0:T(8,128)(2,1)S(1)} %collective-permute-done.2.refs_7_), channel_id=1, source_target_pairs={{0,1},{1,0},{2,3},{3,2},{4,5},{5,4},{6,7},{7,6},{8,9},{9,8},{10,11... | collective-permute-start | bytes 2359304 | tf_op jit(solution)/shard_map/ppermute | solution.py:17
  89.7 19.1 %collective-permute-start.9 = (bf16[4,48,2048]{2,1,0:T(8,128)(2,1)}, bf16[4,48,2048]{2,1,0:T(8,128)(2,1)S(1)}, u32[]{:S(2)}, u32[]{:S(2)}) collective-permute-start(bf16[4,48,2048]{2,1,0:T(8,128)(2,1)} %collective-permute-done.1.refs_6_), channel_id=1, source_target_pairs={{0,1},{1,0},{2,3},{3,2},{4,5},{5,4},{6,7},{7,6},{8,9},{9,8},{10,11... | collective-permute-start | bytes 2359304 | tf_op jit(solution)/shard_map/ppermute | solution.py:17
  90.2 21.8 %collective-permute-start.5 = (bf16[4,48,2048]{2,1,0:T(8,128)(2,1)}, bf16[4,48,2048]{2,1,0:T(8,128)(2,1)S(1)}, u32[]{:S(2)}, u32[]{:S(2)}) collective-permute-start(bf16[4,48,2048]{2,1,0:T(8,128)(2,1)} %collective-permute-done.1.refs_6_), channel_id=1, source_target_pairs={{0,2},{2,4},{4,6},{6,0},{1,3},{3,5},{5,7},{7,1},{8,10},{10,12},{12... | collective-permute-start | bytes 2359304 | tf_op jit(solution)/shard_map/ppermute | solution.py:21
  90.9 17.8 %copy-start.5 = (bf16[4,48,2048]{2,1,0:T(8,128)(2,1)}, bf16[4,48,2048]{2,1,0:T(8,128)(2,1)S(1)}, u32[]{:S(2)}) copy-start(bf16[4,48,2048]{2,1,0:T(8,128)(2,1)S(1)} %collective-permute-done.7.refs_12_) | copy-start | bytes 2359300
  90.9 37.1 %collective-permute-start.3 = (bf16[4,48,2048]{2,1,0:T(8,128)(2,1)}, bf16[4,48,2048]{2,1,0:T(8,128)(2,1)S(1)}, u32[]{:S(2)}, u32[]{:S(2)}) collective-permute-start(bf16[4,48,2048]{2,1,0:T(8,128)(2,1)} %collective-permute-done.refs_5_), channel_id=1, source_target_pairs={{0,2},{2,4},{4,6},{6,0},{1,3},{3,5},{5,7},{7,1},{8,10},{10,12},{12... | collective-permute-start | bytes 2359304 | tf_op jit(solution)/shard_map/ppermute | solution.py:21
  105.1 22.8 %collective-permute-start.6 = (bf16[4,48,2048]{2,1,0:T(8,128)(2,1)S(1)}, bf16[4,48,2048]{2,1,0:T(8,128)(2,1)}, u32[]{:S(2)}, u32[]{:S(2)}) collective-permute-start(bf16[4,48,2048]{2,1,0:T(8,128)(2,1)S(1)} %collective-permute-done.4.refs_9_), channel_id=1, source_target_pairs={{0,6},{2,0},{4,2},{6,4},{1,7},{3,1},{5,3},{7,5},{8,14},{10,8},{12,... | collective-permute-start | bytes 2359304 | tf_op jit(solution)/shard_map/ppermute | solution.py:21
  108.7 19.8 %copy-start.7 = (bf16[4,48,2048]{2,1,0:T(8,128)(2,1)}, bf16[4,48,2048]{2,1,0:T(8,128)(2,1)S(1)}, u32[]{:S(2)}) copy-start(bf16[4,48,2048]{2,1,0:T(8,128)(2,1)S(1)} %collective-permute-done.10.refs_15_) | copy-start | bytes 2359300
  108.7 19.7 %collective-permute-start.8 = (bf16[4,48,2048]{2,1,0:T(8,128)(2,1)}, bf16[4,48,2048]{2,1,0:T(8,128)(2,1)S(1)}, u32[]{:S(2)}, u32[]{:S(2)}) collective-permute-start(bf16[4,48,2048]{2,1,0:T(8,128)(2,1)} %collective-permute-done.refs_5_), channel_id=1, source_target_pairs={{0,1},{1,0},{2,3},{3,2},{4,5},{5,4},{6,7},{7,6},{8,9},{9,8},{10,11... | collective-permute-start | bytes 2359304 | tf_op jit(solution)/shard_map/ppermute | solution.py:17
  108.8 19.7 %copy-start.8 = (bf16[4,48,2048]{2,1,0:T(8,128)(2,1)}, bf16[4,48,2048]{2,1,0:T(8,128)(2,1)S(1)}, u32[]{:S(2)}) copy-start(bf16[4,48,2048]{2,1,0:T(8,128)(2,1)S(1)} %collective-permute-done.9.refs_14_) | copy-start | bytes 2359300
  108.8 19.6 %collective-permute-start.12 = (bf16[4,48,2048]{2,1,0:T(8,128)(2,1)S(1)}, bf16[4,48,2048]{2,1,0:T(8,128)(2,1)S(1)}, u32[]{:S(2)}, u32[]{:S(2)}) collective-permute-start(bf16[4,48,2048]{2,1,0:T(8,128)(2,1)S(1)} %collective-permute-done.4.refs_9_), channel_id=1, source_target_pairs={{0,1},{1,0},{2,3},{3,2},{4,5},{5,4},{6,7},{7,6},{8,9},{9,8},{10,11... | collective-permute-start | bytes 2359304 | tf_op jit(solution)/shard_map/ppermute | solution.py:17
  112.0 16.5 %copy-start.9 = (bf16[4,48,2048]{2,1,0:T(8,128)(2,1)}, bf16[4,48,2048]{2,1,0:T(8,128)(2,1)S(1)}, u32[]{:S(2)}) copy-start(bf16[4,48,2048]{2,1,0:T(8,128)(2,1)S(1)} %collective-permute-done.5.refs_10_) | copy-start | bytes 2359300
  112.0 16.4 %collective-permute-start.13 = (bf16[4,48,2048]{2,1,0:T(8,128)(2,1)S(1)}, bf16[4,48,2048]{2,1,0:T(8,128)(2,1)S(1)}, u32[]{:S(2)}, u32[]{:S(2)}) collective-permute-start(bf16[4,48,2048]{2,1,0:T(8,128)(2,1)S(1)} %collective-permute-done.5.refs_10_), channel_id=1, source_target_pairs={{0,1},{1,0},{2,3},{3,2},{4,5},{5,4},{6,7},{7,6},{8,9},{9,8},{10,11... | collective-permute-start | bytes 2359304 | tf_op jit(solution)/shard_map/ppermute | solution.py:17
  127.9 2.6 %collective-permute-start.11 = (bf16[4,48,2048]{2,1,0:T(8,128)(2,1)S(1)}, bf16[4,48,2048]{2,1,0:T(8,128)(2,1)}, u32[]{:S(2)}, u32[]{:S(2)}) collective-permute-start(bf16[4,48,2048]{2,1,0:T(8,128)(2,1)S(1)} %collective-permute-done.3.refs_8_), channel_id=1, source_target_pairs={{0,1},{1,0},{2,3},{3,2},{4,5},{5,4},{6,7},{7,6},{8,9},{9,8},{10,11... | collective-permute-start | bytes 2359304 | tf_op jit(solution)/shard_map/ppermute | solution.py:17
  127.9 3.5 %collective-permute-start.14 = (bf16[4,48,2048]{2,1,0:T(8,128)(2,1)}, bf16[4,48,2048]{2,1,0:T(8,128)(2,1)}, u32[]{:S(2)}, u32[]{:S(2)}) collective-permute-start(bf16[4,48,2048]{2,1,0:T(8,128)(2,1)} %collective-permute-done.6.refs_11_), channel_id=1, source_target_pairs={{0,1},{1,0},{2,3},{3,2},{4,5},{5,4},{6,7},{7,6},{8,9},{9,8},{10,11... | collective-permute-start | bytes 2359304 | tf_op jit(solution)/shard_map/ppermute | solution.py:17
  (7 other events, 18.5 us)
where the time goes:
time: 162 us; the launch traced here: 161 us
  waiting for transfers between devices  85.9 us (53%)
  Pallas kernels  31.7 us (20%)
  starting transfers between devices  27 us (17%)
  local copies, waits for them, and re-layouts  7.44 us (5%)
  matrix products  7.01 us (4%)
    ppermute x6, waiting for transfers between devices, shift(): return lax.ppermute(value, 'x', [(i, (i + step) % 4) for i in range(4)])  46.1 us
    all_to_all x1, waiting for transfers between devices, shards(): lax.all_to_all(rows.reshape(orbs * NWIDE, part, cols), ALL, 0, 0, tiled=T...  36 us
    pallas_call x1, Pallas kernels, pair_terms(): pl.pallas_call(body, out_shape=jax.ShapeDtypeStruct((virt, aux), jnp.floa...  29 us
    all_to_all x1, starting transfers between devices, shards(): lax.all_to_all(rows.reshape(orbs * NWIDE, part, cols), ALL, 0, 0, tiled=T...  11.6 us
    ppermute x6, starting transfers between devices, shift(): return lax.ppermute(value, 'x', [(i, (i + step) % 4) for i in range(4)])  8.29 us
    dot_general x1, matrix products, shards(): jnp.einsum('imp,ma->iap', half_integrals[0], coeff_virtual, preferred_ele...  7.01 us
    all_to_all x1, starting transfers between devices, shards(): rows_i = lax.all_to_all(rows, GRP, 0, 0, tiled=True)  4.46 us
    ppermute x9, waiting for transfers between devices, swap(): return lax.ppermute(value, axis, [(0, 1), (1, 0)])  3.87 us
  transfers between devices with their start and end apart: 17, of which 8 were waited for; matrix products, arithmetic and copies ran while one was open for 3% of the time, Pallas kernels for 0%

commit v1 on v0

--- a/solution.py
+++ b/solution.py
@@ -25,23 +25,26 @@
     other = swap(own, "yhi")
     own_r = shift(own, 1)
     own_l = shift(own, -1)
-    other, own_r, own_l = lax.optimization_barrier((other, own_r, own_l))
     oth_l = shift(other, -1)
     oth_r = shift(other, 1)
     own_far = shift(own_r, 1)
     oth_far = shift(oth_l, -1)
     mine = [own, other, own_r, own_l, oth_r, oth_l, own_far, oth_far]
-    return mine + [swap(block, "core") for block in mine]
-
-
-def pick_kernel(plan_ref, spread_ref, out_ref, sem):
+    out = list(mine)
+    for block in mine:
+        out.append(swap(block, "core"))
+    return out
+
+
+def pick_kernel(plan_ref, spread_ref, out_a, out_b, sem):
     cols = spread_ref.shape[3]
     copies = []
     for k in range(4):
         owner = plan_ref[k // 2, k % 2]
+        out_ref = (out_a, out_b)[k // 2]
         for g in range(NGRP):
             copies.append(pltpu.make_async_copy(
-                spread_ref.at[g, owner], out_ref.at[k, :, pl.ds(g * cols, cols)], sem))
+                spread_ref.at[g, owner], out_ref.at[k % 2, :, pl.ds(g * cols, cols)], sem))
     for c in copies:
         c.start()
     for c in copies:
@@ -52,9 +55,9 @@
     part, cols = spread.shape[2:]
     return pl.pallas_call(
         pick_kernel,
-        out_shape=jax.ShapeDtypeStruct((4, part, NGRP * cols), spread.dtype),
+        out_shape=(jax.ShapeDtypeStruct((2, part, NGRP * cols), spread.dtype),) * 2,
         in_specs=[pl.BlockSpec(memory_space=pltpu.SMEM), pl.BlockSpec(memory_space=pl.ANY)],
-        out_specs=pl.BlockSpec(memory_space=pltpu.VMEM),
+        out_specs=(pl.BlockSpec(memory_space=pltpu.VMEM),) * 2,
         scratch_shapes=[pltpu.SemaphoreType.DMA],
         name="pick_owners",
     )(plan, spread)
@@ -70,10 +73,13 @@
     return jnp.stack(out).astype(jnp.int32)
 
 
-def pair_kernel(count, *refs):
+def pair_kernel(count, has_acc, *refs):
     where_ref, energy_ref, vir_ref, rows_i_ref = refs[:4]
     blocks = refs[4:4 + NWIDE]
-    out_ref, rows_i, rows_j, amp, comb, obuf, in_sem, out_sem = refs[4 + NWIDE:]
+    refs = refs[4 + NWIDE:]
+    if has_acc:
+        acc_ref, refs = refs[0], refs[1:]
+    out_ref, rows_i, rows_j, amp, comb, obuf, abuf, in_sem, out_sem, acc_sem = refs
     virt, aux = rows_i.shape
     part = blocks[0].shape[1]
     wide_p = rows_i_ref.shape[2]
@@ -96,6 +102,12 @@
         return pltpu.make_async_copy(
             obuf.at[n % 2], out_ref.at[:, pl.ds(n * step, step)], out_sem.at[n % 2])
 
+    def acc_copy(n):
+        return pltpu.make_async_copy(
+            acc_ref.at[:, pl.ds(n * step, step)], abuf.at[n % 2], acc_sem.at[n % 2])
+
+    if has_acc:
+        acc_copy(0).start()
     vrow = vir_ref[...]
     vcol = jnp.broadcast_to(vrow, (128, virt)).T[:, :1]
     tile = 256
@@ -113,8 +125,13 @@
                 comb[i * tile:(i + 1) * tile, k * virt + j * tile:k * virt + (j + 1) * tile] = (
                     2.0 * here - there.T).astype(jnp.bfloat16)
     for n in range(nstep):
+        if has_acc and n + 1 < nstep:
+            acc_copy(n + 1).start()
         total = jnp.dot(comb[...], rows_j[:, n * step:(n + 1) * step],
                         preferred_element_type=jnp.float32)
+        if has_acc:
+            acc_copy(n).wait()
+            total = total + abuf[n % 2]
         if n >= 2:
             out_copy(n - 2).wait()
         obuf[n % 2] = total
@@ -123,7 +140,7 @@
         out_copy(n).wait()
 
 
-def pair_terms(where, energies, vir, rows_i, blocks):
+def pair_terms(where, energies, vir, rows_i, blocks, acc):
     count, _, aux = blocks[0].shape
     virt = rows_i.shape[1]
     step = 512
@@ -131,13 +148,15 @@
     smem = pl.BlockSpec(memory_space=pltpu.SMEM)
     vmem = pl.BlockSpec(memory_space=pltpu.VMEM)
 
+    args = [where, energies, vir, rows_i, *blocks] + ([] if acc is None else [acc])
+
     def body(*refs):
-        pair_kernel(count, *refs)
+        pair_kernel(count, acc is not None, *refs)
 
     return pl.pallas_call(
         body,
         out_shape=jax.ShapeDtypeStruct((virt, aux), jnp.float32),
-        in_specs=[smem, smem, vmem] + [anyspec] * (1 + NWIDE),
+        in_specs=[smem, smem, vmem] + [anyspec] * (len(args) - 3),
         out_specs=anyspec,
         scratch_shapes=[
             pltpu.VMEM((virt, aux), jnp.bfloat16),
@@ -145,15 +164,16 @@
             pltpu.VMEM((virt, virt), jnp.float32),
             pltpu.VMEM((virt, count * virt), jnp.bfloat16),
             pltpu.VMEM((2, virt, step), jnp.float32),
+            pltpu.VMEM((2, virt, step), jnp.float32),
             pltpu.SemaphoreType.DMA((count,)),
+            pltpu.SemaphoreType.DMA((2,)),
             pltpu.SemaphoreType.DMA((2,)),
         ],
         compiler_params=pltpu.CompilerParams(vmem_limit_bytes=56 * 1024 * 1024),
         cost_estimate=pl.CostEstimate(
             flops=4 * count * virt * virt * aux, transcendentals=0,
             bytes_accessed=2 * (count + 1) * virt * aux + 4 * virt * aux),
-        name="pair_terms",
-    )(where, energies, vir, rows_i, *blocks)
+    )(*args)
 
 
 def shards(half_integrals, coeff_virtual, occ_energy, vir_energy, plan):
@@ -170,12 +190,16 @@
     energy = lax.dynamic_slice_in_dim(occ_energy, grp, 1, 1)[:, 0]
     my_energy = lax.dynamic_slice_in_dim(energy, wide, 1)
     e_own = jnp.take(energy, owners, axis=0)
-    small = (block_indices(), jnp.concatenate([my_energy, e_own]), vir_energy[None, :])
-    spread, (where, energies, vrow) = lax.optimization_barrier((spread, small))
-    picked, rows = lax.optimization_barrier((pick_owners(plan, spread), rows))
-    blocks = gather_wide(picked)
+    small = (block_indices(), jnp.concatenate([my_energy, e_own[:2]]),
+             jnp.concatenate([my_energy, e_own[2:]]), vir_energy[None, :])
+    spread, (where, e_first, e_second, vrow) = lax.optimization_barrier((spread, small))
+    (first, second), rows = lax.optimization_barrier((pick_owners(plan, spread), rows))
+    first = gather_wide(first)
+    second = gather_wide(second)
     rows_i = lax.all_to_all(rows, GRP, 0, 0, tiled=True)
-    return pair_terms(where, energies, vrow, rows_i, blocks)[None, None]
+    density = pair_terms(where, e_first, vrow, rows_i, first, None)
+    density = pair_terms(where, e_second, vrow, rows_i, second, density)
+    return density[None, None]
 
 
 def solution(mesh):

time: 162 us -> 214 us (1.32)
  waiting for transfers between devices: 85.9 us -> 121 us
  starting transfers between devices: 27 us -> 37.4 us
  Pallas kernels: 31.7 us -> 38.1 us
    ppermute x9 -> x18, waiting for transfers between devices: 3.87 us -> 43 us  [swap(): return lax.ppermute(value, axis, [(0, 1), (1, 0)])]
    pallas_call x1 -> x2, Pallas kernels: 29 us -> 35.4 us  [pair_terms(): pl.pallas_call(body, out_shape=jax.ShapeDtypeStruct((virt, aux), jnp.floa...]
    ppermute x6 -> x12, starting transfers between devices: 8.29 us -> 14.3 us  [shift(): return lax.ppermute(value, 'x', [(i, (i + step) % 4) for i in range(4)])]
    ppermute x9 -> x18, starting transfers between devices: 2.64 us -> 6.87 us  [swap(): return lax.ppermute(value, axis, [(0, 1), (1, 0)])]
    ppermute x6 -> x12, waiting for transfers between devices: 46.1 us -> 42.6 us  [shift(): return lax.ppermute(value, 'x', [(i, (i + step) % 4) for i in range(4)])]
  transfers between devices with their start and end apart: 17 -> 32, of which waited for: 8 -> 13; matrix products, arithmetic and copies ran while one was open for 3% -> 3% of each run, Pallas kernels for 0% -> 8%
where the time goes in v1:
time: 214 us; the launch traced here: 212 us
  waiting for transfers between devices  121 us (57%)
  Pallas kernels  38.1 us (18%)
  starting transfers between devices  37.4 us (17%)
  matrix products  7.01 us (3%)
  local copies, waits for them, and re-layouts  6.3 us (3%)
    ppermute x18, waiting for transfers between devices, swap(): return lax.ppermute(value, axis, [(0, 1), (1, 0)])  43 us
    ppermute x12, waiting for transfers between devices, shift(): return lax.ppermute(value, 'x', [(i, (i + step) % 4) for i in range(4)])  42.6 us
    all_to_all x1, waiting for transfers between devices, shards(): lax.all_to_all(rows.reshape(orbs * NWIDE, part, cols), ALL, 0, 0, tiled=T...  35.8 us
    pallas_call x2, Pallas kernels, pair_terms(): pl.pallas_call(body, out_shape=jax.ShapeDtypeStruct((virt, aux), jnp.floa...  35.4 us
    ppermute x12, starting transfers between devices, shift(): return lax.ppermute(value, 'x', [(i, (i + step) % 4) for i in range(4)])  14.3 us
    all_to_all x1, starting transfers between devices, shards(): lax.all_to_all(rows.reshape(orbs * NWIDE, part, cols), ALL, 0, 0, tiled=T...  11.6 us
    dot_general x1, matrix products, shards(): jnp.einsum('imp,ma->iap', half_integrals[0], coeff_virtual, preferred_ele...  7.01 us
    ppermute x18, starting transfers between devices, swap(): return lax.ppermute(value, axis, [(0, 1), (1, 0)])  6.87 us
  transfers between devices with their start and end apart: 32, of which 13 were waited for; matrix products, arithmetic and copies ran while one was open for 3% of the time, Pallas kernels for 8%

profile of v1, /device:TPU:0, one launch (start us, length us, event | category | flops | bytes accessed | tf_op | source)
XLA Modules:
  0.0 212.2 jit_solution(14180762048606956647)
XLA Ops:
  0.0 1.4 copy-done
  1.4 7.0 %fusion.2 = bf16[768,8,256]{2,0,1:T(8,128)(2,1)} fusion(bf16[1,8,1024,256]{3,2,1,0:T(8,128)(2,1)} %param.5, bf16[1024,768]{1,0:T(8,128)(2,1)S(1)} %copy-done), kind=kOutput, calls=%fused_computation.3 | convolution fusion | flops 3222798336 | bytes 8912896 | tf_op jit(solution)/shard_map/imp,ma->iap/dot_general | solution.py:180
  8.4 11.6 %all-to-all-start = ((bf16[128,48,256]{2,1,0:T(8,128)(2,1)}), bf16[128,48,256]{2,1,0:T(8,128)(2,1)}, u32[]{:S(2)}, u32[]{:S(2)}) async-start(bf16[128,48,256]{2,1,0:T(8,128)(2,1)} %bitcast.34), calls=%async_computation | async-start | bytes 6291456 | tf_op jit(solution)/shard_map/all_to_all | solution.py:185
  20.9 1.3 dynamic_slice.8
  24.2 1.3 pad_maximum_fusion
  25.5 35.8 %all-to-all-done = bf16[128,48,256]{2,1,0:T(8,128)(2,1)} async-done(((bf16[128,48,256]{2,1,0:T(8,128)(2,1)}), bf16[128,48,256]{2,1,0:T(8,128)(2,1)}, u32[]{:S(2)}, u32[]{:S(2)}) %all-to-all-start) | async-done | bytes 3145760 | tf_op jit(solution)/shard_map/all_to_all | solution.py:185
  61.3 2.7 %pick_owners.1 = (bf16[2,48,2048]{2,1,0:T(8,128)(2,1)}, bf16[2,48,2048]{2,1,0:T(8,128)(2,1)}) custom-call(s32[2,2]{1,0:T(2,128)} %plan_ref.1, bf16[8,16,48,256]{3,2,1,0:T(8,128)(2,1)} %bitcast.4.spread_ref), custom_call_target="tpu_custom_call" | custom-call | tf_op jit(solution)/shard_map/pick_owners/pallas_call | solution.py:56
  64.0 4.6 %all-to-all-start.1 = ((bf16[8,768,256]{2,1,0:T(8,128)(2,1)}), bf16[8,768,256]{2,1,0:T(8,128)(2,1)}, u32[]{:S(2)}, u32[]{:S(2)}) async-start(bf16[8,768,256]{2,1,0:T(8,128)(2,1)} %bitcast.35), calls=%async_computation.1 | async-start | bytes 6291456 | tf_op jit(solution)/shard_map/all_to_all | solution.py:199
  70.3 2.3 %collective-permute-start.17 = (bf16[2,48,2048]{2,1,0:T(8,128)(2,1)S(1)}, bf16[2,48,2048]{2,1,0:T(8,128)(2,1)S(1)}, u32[]{:S(2)}, u32[]{:S(2)}) collective-permute-start(bf16[2,48,2048]{2,1,0:T(8,128)(2,1)S(1)} %copy-done.6), channel_id=1, source_target_pairs={{0,6},{2,0},{4,2},{6,4},{1,7},{3,1},{5,3},{7,5},{8,14},{10,8},{12,... | collective-permute-start | bytes 1179656 | tf_op jit(solution)/shard_map/ppermute | solution.py:21
  72.8 2.6 %collective-permute-start = (bf16[2,48,2048]{2,1,0:T(8,128)(2,1)S(1)}, bf16[2,48,2048]{2,1,0:T(8,128)(2,1)S(1)}, u32[]{:S(2)}, u32[]{:S(2)}) collective-permute-start(bf16[2,48,2048]{2,1,0:T(8,128)(2,1)S(1)} %copy-done.3), channel_id=1, source_target_pairs={{0,8},{8,0},{1,9},{9,1},{2,10},{10,2},{3,11},{11,3},{4,12},{12,4},... | collective-permute-start | bytes 1179656 | tf_op jit(solution)/shard_map/ppermute | solution.py:17
  75.5 37.5 %collective-permute-done.15.refs_5_ = bf16[2,48,2048]{2,1,0:T(8,128)(2,1)S(1)} collective-permute-done((bf16[2,48,2048]{2,1,0:T(8,128)(2,1)S(1)}, bf16[2,48,2048]{2,1,0:T(8,128)(2,1)S(1)}, u32[]{:S(2)}, u32[]{:S(2)}) %collective-permute-start.15) | collective-permute-done | bytes 393248 | tf_op jit(solution)/shard_map/ppermute | solution.py:17
  114.1 2.0 collective-permute-start.2
  116.7 4.6 %collective-permute-done.refs_5_ = bf16[2,48,2048]{2,1,0:T(8,128)(2,1)S(1)} collective-permute-done((bf16[2,48,2048]{2,1,0:T(8,128)(2,1)S(1)}, bf16[2,48,2048]{2,1,0:T(8,128)(2,1)S(1)}, u32[]{:S(2)}, u32[]{:S(2)}) %collective-permute-start) | collective-permute-done | bytes 393248 | tf_op jit(solution)/shard_map/ppermute | solution.py:17
  122.2 3.9 %collective-permute-done.1.refs_6_ = bf16[2,48,2048]{2,1,0:T(8,128)(2,1)S(1)} collective-permute-done((bf16[2,48,2048]{2,1,0:T(8,128)(2,1)S(1)}, bf16[2,48,2048]{2,1,0:T(8,128)(2,1)S(1)}, u32[]{:S(2)}, u32[]{:S(2)}) %collective-permute-start.1) | collective-permute-done | bytes 393248 | tf_op jit(solution)/shard_map/ppermute | solution.py:21
  126.7 6.8 %collective-permute-done.19.refs_9_ = bf16[2,48,2048]{2,1,0:T(8,128)(2,1)S(1)} collective-permute-done((bf16[2,48,2048]{2,1,0:T(8,128)(2,1)S(1)}, bf16[2,48,2048]{2,1,0:T(8,128)(2,1)S(1)}, u32[]{:S(2)}, u32[]{:S(2)}) %collective-permute-start.19) | collective-permute-done | bytes 393248 | tf_op jit(solution)/shard_map/ppermute | solution.py:21
  134.5 2.8 %collective-permute-start.4 = (bf16[2,48,2048]{2,1,0:T(8,128)(2,1)S(1)}, bf16[2,48,2048]{2,1,0:T(8,128)(2,1)S(1)}, u32[]{:S(2)}, u32[]{:S(2)}) collective-permute-start(bf16[2,48,2048]{2,1,0:T(8,128)(2,1)S(1)} %collective-permute-done.refs_5_), channel_id=1, source_target_pairs={{0,6},{2,0},{4,2},{6,4},{1,7},{3,1},{5,3},{7,5},{8,14},{10,8},{12,... | collective-permute-start | bytes 1179656 | tf_op jit(solution)/shard_map/ppermute | solution.py:21
  137.4 5.4 %collective-permute-done.20.refs_10_ = bf16[2,48,2048]{2,1,0:T(8,128)(2,1)S(1)} collective-permute-done((bf16[2,48,2048]{2,1,0:T(8,128)(2,1)S(1)}, bf16[2,48,2048]{2,1,0:T(8,128)(2,1)S(1)}, u32[]{:S(2)}, u32[]{:S(2)}) %collective-permute-start.20) | collective-permute-done | bytes 393248 | tf_op jit(solution)/shard_map/ppermute | solution.py:21
  143.5 2.9 %collective-permute-done.4.refs_9_ = bf16[2,48,2048]{2,1,0:T(8,128)(2,1)S(1)} collective-permute-done((bf16[2,48,2048]{2,1,0:T(8,128)(2,1)S(1)}, bf16[2,48,2048]{2,1,0:T(8,128)(2,1)S(1)}, u32[]{:S(2)}, u32[]{:S(2)}) %collective-permute-start.4) | collective-permute-done | bytes 393248 | tf_op jit(solution)/shard_map/ppermute | solution.py:21
  146.3 3.7 %collective-permute-start.21 = (bf16[2,48,2048]{2,1,0:T(8,128)(2,1)S(1)}, bf16[2,48,2048]{2,1,0:T(8,128)(2,1)S(1)}, u32[]{:S(2)}, u32[]{:S(2)}) collective-permute-start(bf16[2,48,2048]{2,1,0:T(8,128)(2,1)S(1)} %collective-permute-done.19.refs_9_), channel_id=1, source_target_pairs={{0,6},{2,0},{4,2},{6,4},{1,7},{3,1},{5,3},{7,5},{8,14},{10,8},{12,... | collective-permute-start | bytes 1179656 | tf_op jit(solution)/shard_map/ppermute | solution.py:21
  150.0 6.0 %collective-permute-done.3.refs_8_ = bf16[2,48,2048]{2,1,0:T(8,128)(2,1)} collective-permute-done((bf16[2,48,2048]{2,1,0:T(8,128)(2,1)S(1)}, bf16[2,48,2048]{2,1,0:T(8,128)(2,1)}, u32[]{:S(2)}, u32[]{:S(2)}) %collective-permute-start.3) | collective-permute-done | bytes 393248 | tf_op jit(solution)/shard_map/ppermute | solution.py:21
  156.0 7.3 %collective-permute-done.5.refs_10_ = bf16[2,48,2048]{2,1,0:T(8,128)(2,1)} collective-permute-done((bf16[2,48,2048]{2,1,0:T(8,128)(2,1)S(1)}, bf16[2,48,2048]{2,1,0:T(8,128)(2,1)}, u32[]{:S(2)}, u32[]{:S(2)}) %collective-permute-start.5) | collective-permute-done | bytes 393248 | tf_op jit(solution)/shard_map/ppermute | solution.py:21
  165.8 9.3 %collective-permute-done.6.refs_11_ = bf16[2,48,2048]{2,1,0:T(8,128)(2,1)} collective-permute-done((bf16[2,48,2048]{2,1,0:T(8,128)(2,1)S(1)}, bf16[2,48,2048]{2,1,0:T(8,128)(2,1)}, u32[]{:S(2)}, u32[]{:S(2)}) %collective-permute-start.6) | collective-permute-done | bytes 393248 | tf_op jit(solution)/shard_map/ppermute | solution.py:21
  176.5 16.9 %shard_map.55.refs_20_ = f32[768,2048]{1,0:T(8,128)} custom-call(s32[16]{0:T(128)} %stack.67.refs_0_, f32[3]{0:T(128)} %get-tuple-element.23.refs_1_, f32[1,768]{1,0:T(1,128)} %broadcast_in_dim.8.refs_2_, bf16[8,768,256]{2,1,0:T(8,128)(2,1)} %all-to-all-done.1.refs_3_, bf16[2,48,2048]{2,1,0:T(8,128)(2,1)} %get-tuple-element.24.refs_4_, ...), custom_call_target="tpu_custom_call" | custom-call | flops 9663676416 | bytes 15728640 | tf_op jit(solution)/shard_map/pallas_call | solution.py:156
  193.5 18.5 %shard_map.56 = f32[768,2048]{1,0:T(8,128)} custom-call(s32[16]{0:T(128)} %stack.67.refs_0_, f32[3]{0:T(128)} %get-tuple-element.16.refs_1_, f32[1,768]{1,0:T(1,128)} %broadcast_in_dim.8.refs_2_, bf16[8,768,256]{2,1,0:T(8,128)(2,1)} %all-to-all-done.1.refs_3_, bf16[2,48,2048]{2,1,0:T(8,128)(2,1)} %get-tuple-element.22.refs_4_, ...), custom_call_target="tpu_custom_call" | custom-call | flops 9663676416 | bytes 15728640 | tf_op jit(solution)/shard_map/pallas_call | solution.py:156
  (110 shorter events, 13.3 us)
Async XLA Ops:
  8.4 52.9 %all-to-all-start = ((bf16[128,48,256]{2,1,0:T(8,128)(2,1)}), bf16[128,48,256]{2,1,0:T(8,128)(2,1)}, u32[]{:S(2)}, u32[]{:S(2)}) async-start(bf16[128,48,256]{2,1,0:T(8,128)(2,1)} %bitcast.34), calls=%async_computation | async-start | bytes 6291456 | tf_op jit(solution)/shard_map/all_to_all | solution.py:185
  64.0 112.5 %all-to-all-start.1 = ((bf16[8,768,256]{2,1,0:T(8,128)(2,1)}), bf16[8,768,256]{2,1,0:T(8,128)(2,1)}, u32[]{:S(2)}, u32[]{:S(2)}) async-start(bf16[8,768,256]{2,1,0:T(8,128)(2,1)} %bitcast.35), calls=%async_computation.1 | async-start | bytes 6291456 | tf_op jit(solution)/shard_map/all_to_all | solution.py:199
  68.6 44.3 %collective-permute-start.15 = (bf16[2,48,2048]{2,1,0:T(8,128)(2,1)S(1)}, bf16[2,48,2048]{2,1,0:T(8,128)(2,1)S(1)}, u32[]{:S(2)}, u32[]{:S(2)}) collective-permute-start(bf16[2,48,2048]{2,1,0:T(8,128)(2,1)S(1)} %copy-done.6), channel_id=1, source_target_pairs={{0,8},{8,0},{1,9},{9,1},{2,10},{10,2},{3,11},{11,3},{4,12},{12,4},... | collective-permute-start | bytes 1179656 | tf_op jit(solution)/shard_map/ppermute | solution.py:17
  69.3 44.8 %collective-permute-start.16 = (bf16[2,48,2048]{2,1,0:T(8,128)(2,1)S(1)}, bf16[2,48,2048]{2,1,0:T(8,128)(2,1)S(1)}, u32[]{:S(2)}, u32[]{:S(2)}) collective-permute-start(bf16[2,48,2048]{2,1,0:T(8,128)(2,1)S(1)} %copy-done.6), channel_id=1, source_target_pairs={{0,2},{2,4},{4,6},{6,0},{1,3},{3,5},{5,7},{7,1},{8,10},{10,12},{12... | collective-permute-start | bytes 1179656 | tf_op jit(solution)/shard_map/ppermute | solution.py:21
  70.3 45.8 %collective-permute-start.17 = (bf16[2,48,2048]{2,1,0:T(8,128)(2,1)S(1)}, bf16[2,48,2048]{2,1,0:T(8,128)(2,1)S(1)}, u32[]{:S(2)}, u32[]{:S(2)}) collective-permute-start(bf16[2,48,2048]{2,1,0:T(8,128)(2,1)S(1)} %copy-done.6), channel_id=1, source_target_pairs={{0,6},{2,0},{4,2},{6,4},{1,7},{3,1},{5,3},{7,5},{8,14},{10,8},{12,... | collective-permute-start | bytes 1179656 | tf_op jit(solution)/shard_map/ppermute | solution.py:21
  72.6 43.8 %collective-permute-start.22 = (bf16[2,48,2048]{2,1,0:T(8,128)(2,1)S(1)}, bf16[2,48,2048]{2,1,0:T(8,128)(2,1)S(1)}, u32[]{:S(2)}, u32[]{:S(2)}) collective-permute-start(bf16[2,48,2048]{2,1,0:T(8,128)(2,1)S(1)} %copy-done.6), channel_id=1, source_target_pairs={{0,1},{1,0},{2,3},{3,2},{4,5},{5,4},{6,7},{7,6},{8,9},{9,8},{10,11... | collective-permute-start | bytes 1179656 | tf_op jit(solution)/shard_map/ppermute | solution.py:17
  72.8 48.5 %collective-permute-start = (bf16[2,48,2048]{2,1,0:T(8,128)(2,1)S(1)}, bf16[2,48,2048]{2,1,0:T(8,128)(2,1)S(1)}, u32[]{:S(2)}, u32[]{:S(2)}) collective-permute-start(bf16[2,48,2048]{2,1,0:T(8,128)(2,1)S(1)} %copy-done.3), channel_id=1, source_target_pairs={{0,8},{8,0},{1,9},{9,1},{2,10},{10,2},{3,11},{11,3},{4,12},{12,4},... | collective-permute-start | bytes 1179656 | tf_op jit(solution)/shard_map/ppermute | solution.py:17
  112.9 13.2 %collective-permute-start.1 = (bf16[2,48,2048]{2,1,0:T(8,128)(2,1)S(1)}, bf16[2,48,2048]{2,1,0:T(8,128)(2,1)S(1)}, u32[]{:S(2)}, u32[]{:S(2)}) collective-permute-start(bf16[2,48,2048]{2,1,0:T(8,128)(2,1)S(1)} %copy-done.3), channel_id=1, source_target_pairs={{0,2},{2,4},{4,6},{6,0},{1,3},{3,5},{5,7},{7,1},{8,10},{10,12},{12... | collective-permute-start | bytes 1179656 | tf_op jit(solution)/shard_map/ppermute | solution.py:21
  114.1 12.0 %collective-permute-start.2 = (bf16[2,48,2048]{2,1,0:T(8,128)(2,1)S(1)}, bf16[2,48,2048]{2,1,0:T(8,128)(2,1)S(1)}, u32[]{:S(2)}, u32[]{:S(2)}) collective-permute-start(bf16[2,48,2048]{2,1,0:T(8,128)(2,1)S(1)} %copy-done.3), channel_id=1, source_target_pairs={{0,6},{2,0},{4,2},{6,4},{1,7},{3,1},{5,3},{7,5},{8,14},{10,8},{12,... | collective-permute-start | bytes 1179656 | tf_op jit(solution)/shard_map/ppermute | solution.py:21
  116.3 17.2 %collective-permute-start.19 = (bf16[2,48,2048]{2,1,0:T(8,128)(2,1)S(1)}, bf16[2,48,2048]{2,1,0:T(8,128)(2,1)S(1)}, u32[]{:S(2)}, u32[]{:S(2)}) collective-permute-start(bf16[2,48,2048]{2,1,0:T(8,128)(2,1)S(1)} %collective-permute-done.15.refs_5_), channel_id=1, source_target_pairs={{0,6},{2,0},{4,2},{6,4},{1,7},{3,1},{5,3},{7,5},{8,14},{10,8},{12,... | collective-permute-start | bytes 1179656 | tf_op jit(solution)/shard_map/ppermute | solution.py:21
  121.3 13.2 %collective-permute-start.18 = (bf16[2,48,2048]{2,1,0:T(8,128)(2,1)S(1)}, bf16[2,48,2048]{2,1,0:T(8,128)(2,1)S(1)}, u32[]{:S(2)}, u32[]{:S(2)}) collective-permute-start(bf16[2,48,2048]{2,1,0:T(8,128)(2,1)S(1)} %collective-permute-done.15.refs_5_), channel_id=1, source_target_pairs={{0,2},{2,4},{4,6},{6,0},{1,3},{3,5},{5,7},{7,1},{8,10},{10,12},{12... | collective-permute-start | bytes 1179656 | tf_op jit(solution)/shard_map/ppermute | solution.py:21
  126.1 16.6 %collective-permute-start.20 = (bf16[2,48,2048]{2,1,0:T(8,128)(2,1)S(1)}, bf16[2,48,2048]{2,1,0:T(8,128)(2,1)S(1)}, u32[]{:S(2)}, u32[]{:S(2)}) collective-permute-start(bf16[2,48,2048]{2,1,0:T(8,128)(2,1)S(1)} %collective-permute-done.16.refs_6_), channel_id=1, source_target_pairs={{0,2},{2,4},{4,6},{6,0},{1,3},{3,5},{5,7},{7,1},{8,10},{10,12},{12... | collective-permute-start | bytes 1179656 | tf_op jit(solution)/shard_map/ppermute | solution.py:21
  126.1 16.6 %collective-permute-start.23 = (bf16[2,48,2048]{2,1,0:T(8,128)(2,1)S(1)}, bf16[2,48,2048]{2,1,0:T(8,128)(2,1)S(1)}, u32[]{:S(2)}, u32[]{:S(2)}) collective-permute-start(bf16[2,48,2048]{2,1,0:T(8,128)(2,1)S(1)} %collective-permute-done.15.refs_5_), channel_id=1, source_target_pairs={{0,1},{1,0},{2,3},{3,2},{4,5},{5,4},{6,7},{7,6},{8,9},{9,8},{10,11... | collective-permute-start | bytes 1179656 | tf_op jit(solution)/shard_map/ppermute | solution.py:17
  126.2 16.6 %collective-permute-start.24 = (bf16[2,48,2048]{2,1,0:T(8,128)(2,1)S(1)}, bf16[2,48,2048]{2,1,0:T(8,128)(2,1)S(1)}, u32[]{:S(2)}, u32[]{:S(2)}) collective-permute-start(bf16[2,48,2048]{2,1,0:T(8,128)(2,1)S(1)} %collective-permute-done.16.refs_6_), channel_id=1, source_target_pairs={{0,1},{1,0},{2,3},{3,2},{4,5},{5,4},{6,7},{7,6},{8,9},{9,8},{10,11... | collective-permute-start | bytes 1179656 | tf_op jit(solution)/shard_map/ppermute | solution.py:17
  142.7 13.3 %collective-permute-start.3 = (bf16[2,48,2048]{2,1,0:T(8,128)(2,1)S(1)}, bf16[2,48,2048]{2,1,0:T(8,128)(2,1)}, u32[]{:S(2)}, u32[]{:S(2)}) collective-permute-start(bf16[2,48,2048]{2,1,0:T(8,128)(2,1)S(1)} %collective-permute-done.refs_5_), channel_id=1, source_target_pairs={{0,2},{2,4},{4,6},{6,0},{1,3},{3,5},{5,7},{7,1},{8,10},{10,12},{12... | collective-permute-start | bytes 1179656 | tf_op jit(solution)/shard_map/ppermute | solution.py:21
  142.8 20.6 %collective-permute-start.5 = (bf16[2,48,2048]{2,1,0:T(8,128)(2,1)S(1)}, bf16[2,48,2048]{2,1,0:T(8,128)(2,1)}, u32[]{:S(2)}, u32[]{:S(2)}) collective-permute-start(bf16[2,48,2048]{2,1,0:T(8,128)(2,1)S(1)} %collective-permute-done.1.refs_6_), channel_id=1, source_target_pairs={{0,2},{2,4},{4,6},{6,0},{1,3},{3,5},{5,7},{7,1},{8,10},{10,12},{12... | collective-permute-start | bytes 1179656 | tf_op jit(solution)/shard_map/ppermute | solution.py:21
  142.9 20.5 %collective-permute-start.10 = (bf16[2,48,2048]{2,1,0:T(8,128)(2,1)S(1)}, bf16[2,48,2048]{2,1,0:T(8,128)(2,1)S(1)}, u32[]{:S(2)}, u32[]{:S(2)}) collective-permute-start(bf16[2,48,2048]{2,1,0:T(8,128)(2,1)S(1)} %collective-permute-done.2.refs_7_), channel_id=1, source_target_pairs={{0,1},{1,0},{2,3},{3,2},{4,5},{5,4},{6,7},{7,6},{8,9},{9,8},{10,11... | collective-permute-start | bytes 1179656 | tf_op jit(solution)/shard_map/ppermute | solution.py:17
  143.0 20.9 %collective-permute-start.8 = (bf16[2,48,2048]{2,1,0:T(8,128)(2,1)S(1)}, bf16[2,48,2048]{2,1,0:T(8,128)(2,1)S(1)}, u32[]{:S(2)}, u32[]{:S(2)}) collective-permute-start(bf16[2,48,2048]{2,1,0:T(8,128)(2,1)S(1)} %collective-permute-done.refs_5_), channel_id=1, source_target_pairs={{0,1},{1,0},{2,3},{3,2},{4,5},{5,4},{6,7},{7,6},{8,9},{9,8},{10,11... | collective-permute-start | bytes 1179656 | tf_op jit(solution)/shard_map/ppermute | solution.py:17
  146.3 17.6 %collective-permute-start.21 = (bf16[2,48,2048]{2,1,0:T(8,128)(2,1)S(1)}, bf16[2,48,2048]{2,1,0:T(8,128)(2,1)S(1)}, u32[]{:S(2)}, u32[]{:S(2)}) collective-permute-start(bf16[2,48,2048]{2,1,0:T(8,128)(2,1)S(1)} %collective-permute-done.19.refs_9_), channel_id=1, source_target_pairs={{0,6},{2,0},{4,2},{6,4},{1,7},{3,1},{5,3},{7,5},{8,14},{10,8},{12,... | collective-permute-start | bytes 1179656 | tf_op jit(solution)/shard_map/ppermute | solution.py:21
  164.1 29.3 %collective-permute-start.9 = (bf16[2,48,2048]{2,1,0:T(8,128)(2,1)S(1)}, bf16[2,48,2048]{2,1,0:T(8,128)(2,1)}, u32[]{:S(2)}, u32[]{:S(2)}) collective-permute-start(bf16[2,48,2048]{2,1,0:T(8,128)(2,1)S(1)} %collective-permute-done.1.refs_6_), channel_id=1, source_target_pairs={{0,1},{1,0},{2,3},{3,2},{4,5},{5,4},{6,7},{7,6},{8,9},{9,8},{10,11... | collective-permute-start | bytes 1179656 | tf_op jit(solution)/shard_map/ppermute | solution.py:17
  165.1 28.3 %collective-permute-start.12 = (bf16[2,48,2048]{2,1,0:T(8,128)(2,1)S(1)}, bf16[2,48,2048]{2,1,0:T(8,128)(2,1)}, u32[]{:S(2)}, u32[]{:S(2)}) collective-permute-start(bf16[2,48,2048]{2,1,0:T(8,128)(2,1)S(1)} %collective-permute-done.4.refs_9_), channel_id=1, source_target_pairs={{0,1},{1,0},{2,3},{3,2},{4,5},{5,4},{6,7},{7,6},{8,9},{9,8},{10,11... | collective-permute-start | bytes 1179656 | tf_op jit(solution)/shard_map/ppermute | solution.py:17
  165.7 27.8 %collective-permute-start.11 = (bf16[2,48,2048]{2,1,0:T(8,128)(2,1)}, bf16[2,48,2048]{2,1,0:T(8,128)(2,1)}, u32[]{:S(2)}, u32[]{:S(2)}) collective-permute-start(bf16[2,48,2048]{2,1,0:T(8,128)(2,1)} %collective-permute-done.3.refs_8_), channel_id=1, source_target_pairs={{0,1},{1,0},{2,3},{3,2},{4,5},{5,4},{6,7},{7,6},{8,9},{9,8},{10,11... | collective-permute-start | bytes 1179656 | tf_op jit(solution)/shard_map/ppermute | solution.py:17
  175.1 18.3 %collective-permute-start.13 = (bf16[2,48,2048]{2,1,0:T(8,128)(2,1)}, bf16[2,48,2048]{2,1,0:T(8,128)(2,1)}, u32[]{:S(2)}, u32[]{:S(2)}) collective-permute-start(bf16[2,48,2048]{2,1,0:T(8,128)(2,1)} %collective-permute-done.5.refs_10_), channel_id=1, source_target_pairs={{0,1},{1,0},{2,3},{3,2},{4,5},{5,4},{6,7},{7,6},{8,9},{9,8},{10,11... | collective-permute-start | bytes 1179656 | tf_op jit(solution)/shard_map/ppermute | solution.py:17
  176.0 17.5 %collective-permute-start.14 = (bf16[2,48,2048]{2,1,0:T(8,128)(2,1)}, bf16[2,48,2048]{2,1,0:T(8,128)(2,1)}, u32[]{:S(2)}, u32[]{:S(2)}) collective-permute-start(bf16[2,48,2048]{2,1,0:T(8,128)(2,1)} %collective-permute-done.6.refs_11_), channel_id=1, source_target_pairs={{0,1},{1,0},{2,3},{3,2},{4,5},{5,4},{6,7},{7,6},{8,9},{9,8},{10,11... | collective-permute-start | bytes 1179656 | tf_op jit(solution)/shard_map/ppermute | solution.py:17
  (35 other events, 864.4 us)

commit v2 on v0

v2 whole, which is shorter than its diff:
```python
import jax
import jax.numpy as jnp
from jax import lax
from jax.experimental import pallas as pl
from jax.experimental.pallas import tpu as pltpu
from jax.sharding import Mesh, PartitionSpec as P


GRP = ("ylo", "z")
WIDE = ("yhi", "x", "core")
ALL = GRP + WIDE
NWIDE = 16
NGRP = 8


def swap(value, axis):
    return lax.ppermute(value, axis, [(0, 1), (1, 0)])


def shift(value, step):
    return lax.ppermute(value, "x", [(i, (i + step) % 4) for i in range(4)])


def gather_wide(own):
    other = swap(own, "yhi")
    own_r = shift(own, 1)
    own_l = shift(own, -1)
    oth_l = shift(other, -1)
    oth_r = shift(other, 1)
    own_far = shift(own_r, 1)
    oth_far = shift(oth_l, -1)
    mine = [own, other, own_r, own_l, oth_r, oth_l, own_far, oth_far]
    out = list(mine)
    for block in mine:
        out.append(swap(block, "core"))
    return out


def pick_kernel(plan_ref, spread_ref, out_ref, sem):
    cols = spread_ref.shape[3]
    copies = []
    for k in range(4):
        owner = plan_ref[k // 2, k % 2]
        for g in range(NGRP):
            copies.append(pltpu.make_async_copy(
                spread_ref.at[g, owner], out_ref.at[k, :, pl.ds(g * cols, cols)], sem))
    for c in copies:
        c.start()
    for c in copies:
        c.wait()


def pick_owners(plan, spread):
    part, cols = spread.shape[2:]
    return pl.pallas_call(
        pick_kernel,
        out_shape=jax.ShapeDtypeStruct((4, part, NGRP * cols), spread.dtype),
        in_specs=[pl.BlockSpec(memory_space=pltpu.SMEM), pl.BlockSpec(memory_space=pl.ANY)],
        out_specs=pl.BlockSpec(memory_space=pltpu.VMEM),
        scratch_shapes=[pltpu.SemaphoreType.DMA],
        name="pick_owners",
    )(plan, spread)


def block_indices():
    yhi, x, core = (lax.axis_index(a) for a in WIDE)
    places = [(0, 0), (1, 0), (0, 3), (0, 1), (1, 3), (1, 1), (0, 2), (1, 2)]
    out = []
    for flip in (0, 1):
        for dy, dx in places:
            out.append(((yhi ^ dy) * 4 + (x + dx) % 4) * 2 + (core ^ flip))
    return jnp.stack(out).astype(jnp.int32)


def pair_kernel(*refs):
    where_ref, energy_ref, vir_ref = refs[:3]
    own_rows = refs[3:3 + NGRP]
    cuts = refs[3 + NGRP:3 + NGRP + NWIDE], refs[3 + NGRP + NWIDE:3 + NGRP + 2 * NWIDE]
    out_ref, rows_i, rows_j, amp, comb, obuf, in_sem, out_sem = refs[3 + NGRP + 2 * NWIDE:]
    virt, aux = rows_i.shape
    count = cuts[0][0].shape[0]
    wide_p = own_rows[0].shape[1]
    me = where_ref[NWIDE]
    copies = [[] for _ in range(count)]
    for g, source in enumerate(own_rows):
        start = pl.multiple_of((me ^ g) * wide_p, wide_p)
        copies[0].append(pltpu.make_async_copy(
            source, rows_i.at[:, pl.ds(start, wide_p)], in_sem.at[0]))
    for k in range(count):
        base = k * virt
        for blocks in cuts:
            part = blocks[0].shape[1]
            for b in range(NWIDE):
                start = pl.multiple_of(where_ref[b] * part, 16)
                copies[k].append(pltpu.make_async_copy(
                    blocks[b].at[k], rows_j.at[pl.ds(base + start, part), :], in_sem.at[k]))
            base += NWIDE * part
    for group in copies:
        for c in group:
            c.start()
    vrow = vir_ref[...]
    vcol = jnp.broadcast_to(vrow, (128, virt)).T[:, :1]
    tile = 256
    for k in range(count):
        for c in copies[k]:
            c.wait()
        at = k * virt
        inter = lax.dot_general(
            rows_i[...], rows_j[at:at + virt, :], (((1,), (1,)), ((), ())),
            preferred_element_type=jnp.float32)
        amp[...] = inter / ((energy_ref[0] + energy_ref[1 + k]) - vcol - vrow)
        for i in range(0, virt, tile):
            for j in range(0, virt, tile):
                comb[i:i + tile, at + j:at + j + tile] = (
                    2.0 * amp[i:i + tile, j:j + tile] - amp[j:j + tile, i:i + tile].T
                ).astype(jnp.bfloat16)
    step = obuf.shape[2]
    nstep = aux // step

    def out_copy(n):
        return pltpu.make_async_copy(
            obuf.at[n % 2], out_ref.at[:, pl.ds(n * step, step)], out_sem.at[n % 2])

    for n in range(nstep):
        total = jnp.dot(comb[...], rows_j[:, n * step:(n + 1) * step],
                        preferred_element_type=jnp.float32)
        if n >= 2:
            out_copy(n - 2).wait()
        obuf[n % 2] = total
        out_copy(n).start()
    for n in range(max(nstep - 2, 0), nstep):
        out_copy(n).wait()


def pair_terms(where, energies, vir, rows_i, first, second):
    count, _, aux = first[0].shape
    virt = rows_i[0].shape[0]
    step = 512
    anyspec = pl.BlockSpec(memory_space=pl.ANY)
    smem = pl.BlockSpec(memory_space=pltpu.SMEM)
    vmem = pl.BlockSpec(memory_space=pltpu.VMEM)
    args = [where, energies, vir, *rows_i, *first, *second]
    return pl.pallas_call(
        pair_kernel,
        out_shape=jax.ShapeDtypeStruct((virt, aux), jnp.float32),
        in_specs=[smem, smem, vmem] + [anyspec] * (len(args) - 3),
        out_specs=anyspec,
        scratch_shapes=[
            pltpu.VMEM((virt, aux), jnp.bfloat16),
            pltpu.VMEM((count * virt, aux), jnp.bfloat16),
            pltpu.VMEM((virt, virt), jnp.float32),
            pltpu.VMEM((virt, count * virt), jnp.bfloat16),
            pltpu.VMEM((2, virt, step), jnp.float32),
            pltpu.SemaphoreType.DMA((count,)),
            pltpu.SemaphoreType.DMA((2,)),
        ],
        compiler_params=pltpu.CompilerParams(vmem_limit_bytes=56 * 1024 * 1024),
        cost_estimate=pl.CostEstimate(
            flops=4 * count * virt * virt * aux, transcendentals=0,
            bytes_accessed=2 * (count + 1) * virt * aux + 4 * virt * aux),
        name="pair_terms",
    )(*args)


def shards(half_integrals, coeff_virtual, occ_energy, vir_energy, plan):
    half = half_integrals[0]
    virt = coeff_virtual.shape[1]
    cut = virt // 3
    grp = lax.axis_index(GRP)
    wide = lax.axis_index(WIDE)

    def form(coeff):
        return jnp.einsum(
            "imp,ma->iap", half, coeff, preferred_element_type=jnp.float32
        ).astype(jnp.bfloat16)

    def spread_rows(rows):
        orbs, size, cols = rows.shape
        part = size // NWIDE
        out = lax.all_to_all(rows.reshape(orbs * NWIDE, part, cols), ALL, 0, 0, tiled=True)
        return out.reshape(NGRP, NWIDE, part, cols)

    rows_a = form(coeff_virtual[:, :cut])
    spread_a = spread_rows(rows_a)
    rows_b = form(coeff_virtual[:, cut:])
    spread_b = spread_rows(rows_b)
    rows = jnp.concatenate([rows_a, rows_b], axis=1)
    rows_i = []
    for s in range(NGRP):
        piece = lax.dynamic_index_in_dim(rows, grp ^ s, 0, keepdims=False)
        if s:
            piece = lax.ppermute(piece, GRP, [(g, g ^ s) for g in range(NGRP)])
        rows_i.append(piece)
    energy = lax.dynamic_slice_in_dim(occ_energy, grp, 1, 1)[:, 0]
    my_energy = lax.dynamic_slice_in_dim(energy, wide, 1)
    e_own = jnp.take(energy, plan.reshape(-1), axis=0)
    small = (jnp.concatenate([block_indices(), grp[None].astype(jnp.int32)]),
             jnp.concatenate([my_energy, e_own]), vir_energy[None, :])
    spread_b, (where, energies, vrow) = lax.optimization_barrier((spread_b, small))
    first = gather_wide(pick_owners(plan, spread_a))
    second = gather_wide(pick_owners(plan, spread_b))
    density = pair_terms(where, energies, vrow, rows_i, first, second)
    return density[None, None]


def solution(mesh):
    fine = Mesh(mesh.devices.reshape(2, 4, 2, 4, 2), GRP + WIDE)
    return jax.shard_map(
        shards,
        mesh=fine,
        in_specs=(P(WIDE, None, None, GRP), P(), P(), P(), P()),
        out_specs=P(WIDE, GRP, None, None),
        check_vma=False,
    )
```

time: 162 us -> 206 us (1.27)
  starting transfers between devices: 27 us -> 52.4 us
  waiting for transfers between devices: 85.9 us -> 95.4 us
  other arithmetic: 1.18 us -> 5.93 us
  matrix products: 7.01 us -> 10.6 us
  Pallas kernels: 31.7 us -> 33.9 us
    ppermute x0 -> x7, waiting for transfers between devices: none -> 36.8 us  [shards(): piece = lax.ppermute(piece, GRP, [(g, g ^ s) for g in range(NGRP)])]
    all_to_all x2, waiting for transfers between devices: 36 us -> 13.2 us  [spread_rows(): lax.all_to_all(rows.reshape(orbs * NWIDE, part, cols), ALL, 0, 0, tiled=T...]
    ppermute x0 -> x7, starting transfers between devices: none -> 10.8 us  [shards(): piece = lax.ppermute(piece, GRP, [(g, g ^ s) for g in range(NGRP)])]
    ppermute x6 -> x12, starting transfers between devices: 8.29 us -> 17.4 us  [shift(): return lax.ppermute(value, 'x', [(i, (i + step) % 4) for i in range(4)])]
    ppermute x9 -> x18, starting transfers between devices: 2.64 us -> 8.31 us  [swap(): return lax.ppermute(value, axis, [(0, 1), (1, 0)])]
    ppermute x6 -> x12, waiting for transfers between devices: 46.1 us -> 40.8 us  [shift(): return lax.ppermute(value, 'x', [(i, (i + step) % 4) for i in range(4)])]
    squeeze x0 -> x2, other arithmetic: none -> 4.7 us  [shards(): piece = lax.dynamic_index_in_dim(rows, grp ^ s, 0, keepdims=False)]
    dot_general x1 -> x2, matrix products: 7.01 us -> 10.6 us  [form(): jnp.einsum('imp,ma->iap', half, coeff, preferred_element_type=jnp.float32)]
  transfers between devices with their start and end apart: 17 -> 39, of which waited for: 8 -> 17; matrix products, arithmetic and copies ran while one was open for 3% -> 8% of each run, Pallas kernels for 0% -> 2%
where the time goes in v2:
time: 206 us; the launch traced here: 205 us
  waiting for transfers between devices  95.4 us (46%)
  starting transfers between devices  52.4 us (25%)
  Pallas kernels  33.9 us (16%)
  matrix products  10.6 us (5%)
  local copies, waits for them, and re-layouts  6.04 us (3%)
  other arithmetic  5.93 us (3%)
    ppermute x12, waiting for transfers between devices, shift(): return lax.ppermute(value, 'x', [(i, (i + step) % 4) for i in range(4)])  40.8 us
    ppermute x7, waiting for transfers between devices, shards(): piece = lax.ppermute(piece, GRP, [(g, g ^ s) for g in range(NGRP)])  36.8 us
    pallas_call x1, Pallas kernels, pair_terms(): pl.pallas_call(pair_kernel, out_shape=jax.ShapeDtypeStruct((virt, aux), j...  29.1 us
    ppermute x12, starting transfers between devices, shift(): return lax.ppermute(value, 'x', [(i, (i + step) % 4) for i in range(4)])  17.4 us
    all_to_all x2, starting transfers between devices, spread_rows(): lax.all_to_all(rows.reshape(orbs * NWIDE, part, cols), ALL, 0, 0, tiled=T...  15.9 us
    all_to_all x2, waiting for transfers between devices, spread_rows(): lax.all_to_all(rows.reshape(orbs * NWIDE, part, cols), ALL, 0, 0, tiled=T...  13.2 us
    ppermute x7, starting transfers between devices, shards(): piece = lax.ppermute(piece, GRP, [(g, g ^ s) for g in range(NGRP)])  10.8 us
    dot_general x2, matrix products, form(): jnp.einsum('imp,ma->iap', half, coeff, preferred_element_type=jnp.float32)  10.6 us
  transfers between devices with their start and end apart: 39, of which 17 were waited for; matrix products, arithmetic and copies ran while one was open for 8% of the time, Pallas kernels for 2%

profile of v2, /device:TPU:0, one launch (start us, length us, event | category | flops | bytes accessed | tf_op | source)
XLA Modules:
  0.0 204.8 jit_solution(568906758059609498)
XLA Ops:
  0.0 4.7 %fusion.7 = bf16[256,8,256]{2,0,1:T(8,128)(2,1)} fusion(bf16[1,8,1024,256]{3,2,1,0:T(8,128)(2,1)} %param.5, bf16[1024,768]{1,0:T(8,128)(2,1)} %param.6), kind=kOutput, calls=%fused_computation.22 | convolution fusion | flops 1074266112 | bytes 5767168 | tf_op jit(solution)/shard_map/imp,ma->iap/dot_general | solution.py:173
  4.7 11.2 %all-to-all-start.1 = ((bf16[128,16,256]{2,1,0:T(8,128)(2,1)}), bf16[128,16,256]{2,1,0:T(8,128)(2,1)S(1)}, u32[]{:S(2)}, u32[]{:S(2)}) async-start(bf16[128,16,256]{2,1,0:T(8,128)(2,1)} %bitcast.35), calls=%async_computation.1 | async-start | bytes 2097152 | tf_op jit(solution)/shard_map/all_to_all | solution.py:180
  15.9 5.9 %fusion.4 = bf16[512,8,256]{2,0,1:T(8,128)(2,1)} fusion(bf16[1,8,1024,256]{3,2,1,0:T(8,128)(2,1)} %param.5, bf16[1024,768]{1,0:T(8,128)(2,1)S(1)} %copy-done.5), kind=kOutput, calls=%fused_computation.21 | convolution fusion | flops 2148532224 | bytes 7340032 | tf_op jit(solution)/shard_map/imp,ma->iap/dot_general | solution.py:173
  21.8 13.2 %all-to-all-done.1 = bf16[128,16,256]{2,1,0:T(8,128)(2,1)S(1)} async-done(((bf16[128,16,256]{2,1,0:T(8,128)(2,1)}), bf16[128,16,256]{2,1,0:T(8,128)(2,1)S(1)}, u32[]{:S(2)}, u32[]{:S(2)}) %all-to-all-start.1) | async-done | bytes 1048608 | tf_op jit(solution)/shard_map/all_to_all | solution.py:180
  35.0 4.7 %all-to-all-start = ((bf16[128,32,256]{2,1,0:T(8,128)(2,1)}), bf16[128,32,256]{2,1,0:T(8,128)(2,1)S(1)}, u32[]{:S(2)}, u32[]{:S(2)}) async-start(bf16[128,32,256]{2,1,0:T(8,128)(2,1)} %bitcast.3), calls=%async_computation | async-start | bytes 4194304 | tf_op jit(solution)/shard_map/all_to_all | solution.py:180
  41.8 3.8 %collective-permute-start.5 = (bf16[768,256]{1,0:T(8,128)(2,1)}, bf16[768,256]{1,0:T(8,128)(2,1)}, u32[]{:S(2)}, u32[]{:S(2)}) collective-permute-start(bf16[768,256]{1,0:T(8,128)(2,1)} %get-tuple-element.19), channel_id=1, source_target_pairs={{0,96},{16,112},{32,64},{48,80},{64,32},{80,48},{96,0},{112,16},{1... | collective-permute-start | bytes 1179656 | tf_op jit(solution)/shard_map/ppermute | solution.py:192
  46.4 2.6 %fusion.29 = (bf16[768,256]{1,0:T(8,128)(2,1)}, bf16[768,256]{1,0:T(8,128)(2,1)}, bf16[768,256]{1,0:T(8,128)(2,1)}, bf16[768,256]{1,0:T(8,128)(2,1)S(1)}, bf16[7...) fusion(s32[]{:T(128)S(6)} %select_n.113, bf16[8,512,256]{2,1,0:T(8,128)(2,1)} %bitcast.2, ...), kind=kLoop, calls=%fused_computation.42 | loop fusion | flops 4718592 | bytes 5505048 | tf_op jit(solution)/shard_map/jit(dynamic_index_in_dim)/squeeze | solution.py:190
  51.5 3.2 %collective-permute-start.1 = (bf16[768,256]{1,0:T(8,128)(2,1)S(1)}, bf16[768,256]{1,0:T(8,128)(2,1)}, u32[]{:S(2)}, u32[]{:S(2)}) collective-permute-start(bf16[768,256]{1,0:T(8,128)(2,1)S(1)} %get-tuple-element.16), channel_id=1, source_target_pairs={{0,32},{16,48},{32,0},{48,16},{64,96},{80,112},{96,64},{112,80},{1... | collective-permute-start | bytes 1179656 | tf_op jit(solution)/shard_map/ppermute | solution.py:192
  57.1 19.2 %collective-permute-done.5.refs_9_ = bf16[768,256]{1,0:T(8,128)(2,1)} collective-permute-done((bf16[768,256]{1,0:T(8,128)(2,1)}, bf16[768,256]{1,0:T(8,128)(2,1)}, u32[]{:S(2)}, u32[]{:S(2)}) %collective-permute-start.5) | collective-permute-done | bytes 393248 | tf_op jit(solution)/shard_map/ppermute | solution.py:192
  76.5 5.8 %collective-permute-done.4.refs_8_ = bf16[768,256]{1,0:T(8,128)(2,1)} collective-permute-done((bf16[768,256]{1,0:T(8,128)(2,1)}, bf16[768,256]{1,0:T(8,128)(2,1)}, u32[]{:S(2)}, u32[]{:S(2)}) %collective-permute-start.4) | collective-permute-done | bytes 393248 | tf_op jit(solution)/shard_map/ppermute | solution.py:192
  82.2 4.4 %collective-permute-start.9 = (bf16[4,16,2048]{2,1,0:T(8,128)(2,1)}, bf16[4,16,2048]{2,1,0:T(8,128)(2,1)}, u32[]{:S(2)}, u32[]{:S(2)}) collective-permute-start(bf16[4,16,2048]{2,1,0:T(8,128)(2,1)} %pick_owners.2.refs_11_), channel_id=1, source_target_pairs={{0,6},{2,0},{4,2},{6,4},{1,7},{3,1},{5,3},{7,5},{8,14},{10,8},{12,... | collective-permute-start | bytes 786440 | tf_op jit(solution)/shard_map/ppermute | solution.py:21
  86.6 5.3 %collective-permute-done.6.refs_10_ = bf16[768,256]{1,0:T(8,128)(2,1)} collective-permute-done((bf16[768,256]{1,0:T(8,128)(2,1)}, bf16[768,256]{1,0:T(8,128)(2,1)}, u32[]{:S(2)}, u32[]{:S(2)}) %collective-permute-start.6) | collective-permute-done | bytes 393248 | tf_op jit(solution)/shard_map/ppermute | solution.py:192
  96.3 3.9 %collective-permute-done.1.refs_5_ = bf16[768,256]{1,0:T(8,128)(2,1)} collective-permute-done((bf16[768,256]{1,0:T(8,128)(2,1)S(1)}, bf16[768,256]{1,0:T(8,128)(2,1)}, u32[]{:S(2)}, u32[]{:S(2)}) %collective-permute-start.1) | collective-permute-done | bytes 393248 | tf_op jit(solution)/shard_map/ppermute | solution.py:192
  101.8 2.7 %collective-permute-done.2.refs_6_ = bf16[768,256]{1,0:T(8,128)(2,1)} collective-permute-done((bf16[768,256]{1,0:T(8,128)(2,1)S(1)}, bf16[768,256]{1,0:T(8,128)(2,1)}, u32[]{:S(2)}, u32[]{:S(2)}) %collective-permute-start.2) | collective-permute-done | bytes 393248 | tf_op jit(solution)/shard_map/ppermute | solution.py:192
  104.5 3.6 %collective-permute-start.7 = (bf16[4,16,2048]{2,1,0:T(8,128)(2,1)}, bf16[4,16,2048]{2,1,0:T(8,128)(2,1)S(1)}, u32[]{:S(2)}, u32[]{:S(2)}) collective-permute-start(bf16[4,16,2048]{2,1,0:T(8,128)(2,1)} %pick_owners.2.refs_11_), channel_id=1, source_target_pairs={{0,8},{8,0},{1,9},{9,1},{2,10},{10,2},{3,11},{11,3},{4,12},{12,4},... | collective-permute-start | bytes 786440 | tf_op jit(solution)/shard_map/ppermute | solution.py:17
  112.9 2.8 %collective-permute-start.11 = (bf16[4,16,2048]{2,1,0:T(8,128)(2,1)S(1)}, bf16[4,16,2048]{2,1,0:T(8,128)(2,1)}, u32[]{:S(2)}, u32[]{:S(2)}) collective-permute-start(bf16[4,16,2048]{2,1,0:T(8,128)(2,1)S(1)} %collective-permute-done.7.refs_12_), channel_id=1, source_target_pairs={{0,6},{2,0},{4,2},{6,4},{1,7},{3,1},{5,3},{7,5},{8,14},{10,8},{12,... | collective-permute-start | bytes 786440 | tf_op jit(solution)/shard_map/ppermute | solution.py:21
  122.1 2.6 %collective-permute-start.13 = (bf16[4,16,2048]{2,1,0:T(8,128)(2,1)}, bf16[4,16,2048]{2,1,0:T(8,128)(2,1)S(1)}, u32[]{:S(2)}, u32[]{:S(2)}) collective-permute-start(bf16[4,16,2048]{2,1,0:T(8,128)(2,1)} %collective-permute-done.11.refs_16_), channel_id=1, source_target_pairs={{0,6},{2,0},{4,2},{6,4},{1,7},{3,1},{5,3},{7,5},{8,14},{10,8},{12,... | collective-permute-start | bytes 786440 | tf_op jit(solution)/shard_map/ppermute | solution.py:21
  124.7 5.5 %collective-permute-done.10.refs_15_ = bf16[4,16,2048]{2,1,0:T(8,128)(2,1)S(1)} collective-permute-done((bf16[4,16,2048]{2,1,0:T(8,128)(2,1)S(1)}, bf16[4,16,2048]{2,1,0:T(8,128)(2,1)S(1)}, u32[]{:S(2)}, u32[]{:S(2)}) %collective-permute-start.10) | collective-permute-done | bytes 262176 | tf_op jit(solution)/shard_map/ppermute | solution.py:21
  136.1 9.1 %collective-permute-done.24.refs_30_ = bf16[4,32,2048]{2,1,0:T(8,128)(2,1)S(1)} collective-permute-done((bf16[4,32,2048]{2,1,0:T(8,128)(2,1)}, bf16[4,32,2048]{2,1,0:T(8,128)(2,1)S(1)}, u32[]{:S(2)}, u32[]{:S(2)}) %collective-permute-start.24) | collective-permute-done | bytes 524320 | tf_op jit(solution)/shard_map/ppermute | solution.py:21
  145.8 9.0 %collective-permute-done.26.refs_32_ = bf16[4,32,2048]{2,1,0:T(8,128)(2,1)S(1)} collective-permute-done((bf16[4,32,2048]{2,1,0:T(8,128)(2,1)S(1)}, bf16[4,32,2048]{2,1,0:T(8,128)(2,1)S(1)}, u32[]{:S(2)}, u32[]{:S(2)}) %collective-permute-start.26) | collective-permute-done | bytes 524320 | tf_op jit(solution)/shard_map/ppermute | solution.py:21
  154.7 2.5 %collective-permute-start.28 = (bf16[4,32,2048]{2,1,0:T(8,128)(2,1)S(1)}, bf16[4,32,2048]{2,1,0:T(8,128)(2,1)S(1)}, u32[]{:S(2)}, u32[]{:S(2)}) collective-permute-start(bf16[4,32,2048]{2,1,0:T(8,128)(2,1)S(1)} %collective-permute-done.26.refs_32_), channel_id=1, source_target_pairs={{0,6},{2,0},{4,2},{6,4},{1,7},{3,1},{5,3},{7,5},{8,14},{10,8},{12,... | collective-permute-start | bytes 1572872 | tf_op jit(solution)/shard_map/ppermute | solution.py:21
  157.8 3.9 %collective-permute-done.27.refs_33_ = bf16[4,32,2048]{2,1,0:T(8,128)(2,1)S(1)} collective-permute-done((bf16[4,32,2048]{2,1,0:T(8,128)(2,1)S(1)}, bf16[4,32,2048]{2,1,0:T(8,128)(2,1)S(1)}, u32[]{:S(2)}, u32[]{:S(2)}) %collective-permute-start.27) | collective-permute-done | bytes 524320 | tf_op jit(solution)/shard_map/ppermute | solution.py:21
  161.7 10.3 %collective-permute-done.25.refs_31_ = bf16[4,32,2048]{2,1,0:T(8,128)(2,1)S(1)} collective-permute-done((bf16[4,32,2048]{2,1,0:T(8,128)(2,1)S(1)}, bf16[4,32,2048]{2,1,0:T(8,128)(2,1)S(1)}, u32[]{:S(2)}, u32[]{:S(2)}) %collective-permute-start.25) | collective-permute-done | bytes 524320 | tf_op jit(solution)/shard_map/ppermute | solution.py:21
  175.5 29.1 %pair_terms.1 = f32[768,2048]{1,0:T(8,128)} custom-call(s32[17]{0:T(128)} %concatenate.9.refs_0_, f32[5]{0:T(128)} %pad_maximum_fusion.refs_1_, f32[1,768]{1,0:T(1,128)} %broadcast_in_dim.12.refs_2_, bf16[768,256]{1,0:T(8,128)(2,1)} %get-tuple-element.14.refs_3_, bf16[768,256]{1,0:T(8,128)(2,1)} %collective-permute-done.refs_4_, ...), custom_call_target="tpu_custom_call" | custom-call | flops 19327352832 | bytes 22020096 | tf_op jit(solution)/shard_map/pair_terms/pallas_call | solution.py:143
  (130 shorter events, 35.4 us)
Async XLA Ops:
  4.7 30.3 %all-to-all-start.1 = ((bf16[128,16,256]{2,1,0:T(8,128)(2,1)}), bf16[128,16,256]{2,1,0:T(8,128)(2,1)S(1)}, u32[]{:S(2)}, u32[]{:S(2)}) async-start(bf16[128,16,256]{2,1,0:T(8,128)(2,1)} %bitcast.35), calls=%async_computation.1 | async-start | bytes 2097152 | tf_op jit(solution)/shard_map/all_to_all | solution.py:180
  35.0 74.3 %all-to-all-start = ((bf16[128,32,256]{2,1,0:T(8,128)(2,1)}), bf16[128,32,256]{2,1,0:T(8,128)(2,1)S(1)}, u32[]{:S(2)}, u32[]{:S(2)}) async-start(bf16[128,32,256]{2,1,0:T(8,128)(2,1)} %bitcast.3), calls=%async_computation | async-start | bytes 4194304 | tf_op jit(solution)/shard_map/all_to_all | solution.py:180
  41.8 34.5 %collective-permute-start.5 = (bf16[768,256]{1,0:T(8,128)(2,1)}, bf16[768,256]{1,0:T(8,128)(2,1)}, u32[]{:S(2)}, u32[]{:S(2)}) collective-permute-start(bf16[768,256]{1,0:T(8,128)(2,1)} %get-tuple-element.19), channel_id=1, source_target_pairs={{0,96},{16,112},{32,64},{48,80},{64,32},{80,48},{96,0},{112,16},{1... | collective-permute-start | bytes 1179656 | tf_op jit(solution)/shard_map/ppermute | solution.py:192
  45.6 36.6 %collective-permute-start.4 = (bf16[768,256]{1,0:T(8,128)(2,1)}, bf16[768,256]{1,0:T(8,128)(2,1)}, u32[]{:S(2)}, u32[]{:S(2)}) collective-permute-start(bf16[768,256]{1,0:T(8,128)(2,1)} %get-tuple-element.20), channel_id=1, source_target_pairs={{0,80},{16,64},{32,112},{48,96},{64,16},{80,0},{96,48},{112,32},{1... | collective-permute-start | bytes 1179656 | tf_op jit(solution)/shard_map/ppermute | solution.py:192
  49.1 42.9 %collective-permute-start.6 = (bf16[768,256]{1,0:T(8,128)(2,1)}, bf16[768,256]{1,0:T(8,128)(2,1)}, u32[]{:S(2)}, u32[]{:S(2)}) collective-permute-start(bf16[768,256]{1,0:T(8,128)(2,1)} %get-tuple-element.13), channel_id=1, source_target_pairs={{0,112},{16,96},{32,80},{48,64},{64,48},{80,32},{96,16},{112,0},{1... | collective-permute-start | bytes 1179656 | tf_op jit(solution)/shard_map/ppermute | solution.py:192
  49.9 46.5 %collective-permute-start = (bf16[768,256]{1,0:T(8,128)(2,1)}, bf16[768,256]{1,0:T(8,128)(2,1)}, u32[]{:S(2)}, u32[]{:S(2)}) collective-permute-start(bf16[768,256]{1,0:T(8,128)(2,1)} %get-tuple-element.15), channel_id=1, source_target_pairs={{0,16},{16,0},{32,48},{48,32},{64,80},{80,64},{96,112},{112,96},{1... | collective-permute-start | bytes 1179656 | tf_op jit(solution)/shard_map/ppermute | solution.py:192
  51.5 48.7 %collective-permute-start.1 = (bf16[768,256]{1,0:T(8,128)(2,1)S(1)}, bf16[768,256]{1,0:T(8,128)(2,1)}, u32[]{:S(2)}, u32[]{:S(2)}) collective-permute-start(bf16[768,256]{1,0:T(8,128)(2,1)S(1)} %get-tuple-element.16), channel_id=1, source_target_pairs={{0,32},{16,48},{32,0},{48,16},{64,96},{80,112},{96,64},{112,80},{1... | collective-permute-start | bytes 1179656 | tf_op jit(solution)/shard_map/ppermute | solution.py:192
  76.4 28.1 %collective-permute-start.2 = (bf16[768,256]{1,0:T(8,128)(2,1)S(1)}, bf16[768,256]{1,0:T(8,128)(2,1)}, u32[]{:S(2)}, u32[]{:S(2)}) collective-permute-start(bf16[768,256]{1,0:T(8,128)(2,1)S(1)} %get-tuple-element.17), channel_id=1, source_target_pairs={{0,48},{16,32},{32,16},{48,0},{64,112},{80,96},{96,80},{112,64},{1... | collective-permute-start | bytes 1179656 | tf_op jit(solution)/shard_map/ppermute | solution.py:192
  82.2 25.8 %collective-permute-start.9 = (bf16[4,16,2048]{2,1,0:T(8,128)(2,1)}, bf16[4,16,2048]{2,1,0:T(8,128)(2,1)}, u32[]{:S(2)}, u32[]{:S(2)}) collective-permute-start(bf16[4,16,2048]{2,1,0:T(8,128)(2,1)} %pick_owners.2.refs_11_), channel_id=1, source_target_pairs={{0,6},{2,0},{4,2},{6,4},{1,7},{3,1},{5,3},{7,5},{8,14},{10,8},{12,... | collective-permute-start | bytes 786440 | tf_op jit(solution)/shard_map/ppermute | solution.py:21
  92.0 19.7 %collective-permute-start.3 = (bf16[768,256]{1,0:T(8,128)(2,1)S(1)}, bf16[768,256]{1,0:T(8,128)(2,1)}, u32[]{:S(2)}, u32[]{:S(2)}) collective-permute-start(bf16[768,256]{1,0:T(8,128)(2,1)S(1)} %get-tuple-element.18), channel_id=1, source_target_pairs={{0,64},{16,80},{32,96},{48,112},{64,0},{80,16},{96,32},{112,48},{1... | collective-permute-start | bytes 1179656 | tf_op jit(solution)/shard_map/ppermute | solution.py:192
  96.3 19.4 %collective-permute-start.14 = (bf16[4,16,2048]{2,1,0:T(8,128)(2,1)}, bf16[4,16,2048]{2,1,0:T(8,128)(2,1)S(1)}, u32[]{:S(2)}, u32[]{:S(2)}) collective-permute-start(bf16[4,16,2048]{2,1,0:T(8,128)(2,1)} %pick_owners.2.refs_11_), channel_id=1, source_target_pairs={{0,1},{1,0},{2,3},{3,2},{4,5},{5,4},{6,7},{7,6},{8,9},{9,8},{10,11... | collective-permute-start | bytes 786440 | tf_op jit(solution)/shard_map/ppermute | solution.py:17
  100.2 11.4 %collective-permute-start.8 = (bf16[4,16,2048]{2,1,0:T(8,128)(2,1)}, bf16[4,16,2048]{2,1,0:T(8,128)(2,1)S(1)}, u32[]{:S(2)}, u32[]{:S(2)}) collective-permute-start(bf16[4,16,2048]{2,1,0:T(8,128)(2,1)} %pick_owners.2.refs_11_), channel_id=1, source_target_pairs={{0,2},{2,4},{4,6},{6,0},{1,3},{3,5},{5,7},{7,1},{8,10},{10,12},{12... | collective-permute-start | bytes 786440 | tf_op jit(solution)/shard_map/ppermute | solution.py:21
  118.2 16.1 %collective-permute-start.22 = (bf16[4,32,2048]{2,1,0:T(8,128)(2,1)}, bf16[4,32,2048]{2,1,0:T(8,128)(2,1)S(1)}, u32[]{:S(2)}, u32[]{:S(2)}) collective-permute-start(bf16[4,32,2048]{2,1,0:T(8,128)(2,1)} %pick_owners.3.refs_27_), channel_id=1, source_target_pairs={{0,8},{8,0},{1,9},{9,1},{2,10},{10,2},{3,11},{11,3},{4,12},{12,4},... | collective-permute-start | bytes 1572872 | tf_op jit(solution)/shard_map/ppermute | solution.py:17
  130.1 15.0 %collective-permute-start.24 = (bf16[4,32,2048]{2,1,0:T(8,128)(2,1)}, bf16[4,32,2048]{2,1,0:T(8,128)(2,1)S(1)}, u32[]{:S(2)}, u32[]{:S(2)}) collective-permute-start(bf16[4,32,2048]{2,1,0:T(8,128)(2,1)} %pick_owners.3.refs_27_), channel_id=1, source_target_pairs={{0,6},{2,0},{4,2},{6,4},{1,7},{3,1},{5,3},{7,5},{8,14},{10,8},{12,... | collective-permute-start | bytes 1572872 | tf_op jit(solution)/shard_map/ppermute | solution.py:21
  130.1 15.0 %collective-permute-start.23 = (bf16[4,32,2048]{2,1,0:T(8,128)(2,1)}, bf16[4,32,2048]{2,1,0:T(8,128)(2,1)S(1)}, u32[]{:S(2)}, u32[]{:S(2)}) collective-permute-start(bf16[4,32,2048]{2,1,0:T(8,128)(2,1)} %pick_owners.3.refs_27_), channel_id=1, source_target_pairs={{0,2},{2,4},{4,6},{6,0},{1,3},{3,5},{5,7},{7,1},{8,10},{10,12},{12... | collective-permute-start | bytes 1572872 | tf_op jit(solution)/shard_map/ppermute | solution.py:21
  132.8 12.8 %collective-permute-start.29 = (bf16[4,32,2048]{2,1,0:T(8,128)(2,1)}, bf16[4,32,2048]{2,1,0:T(8,128)(2,1)S(1)}, u32[]{:S(2)}, u32[]{:S(2)}) collective-permute-start(bf16[4,32,2048]{2,1,0:T(8,128)(2,1)} %pick_owners.3.refs_27_), channel_id=1, source_target_pairs={{0,1},{1,0},{2,3},{3,2},{4,5},{5,4},{6,7},{7,6},{8,9},{9,8},{10,11... | collective-permute-start | bytes 1572872 | tf_op jit(solution)/shard_map/ppermute | solution.py:17
  134.3 20.4 %collective-permute-start.26 = (bf16[4,32,2048]{2,1,0:T(8,128)(2,1)S(1)}, bf16[4,32,2048]{2,1,0:T(8,128)(2,1)S(1)}, u32[]{:S(2)}, u32[]{:S(2)}) collective-permute-start(bf16[4,32,2048]{2,1,0:T(8,128)(2,1)S(1)} %collective-permute-done.22.refs_28_), channel_id=1, source_target_pairs={{0,6},{2,0},{4,2},{6,4},{1,7},{3,1},{5,3},{7,5},{8,14},{10,8},{12,... | collective-permute-start | bytes 1572872 | tf_op jit(solution)/shard_map/ppermute | solution.py:21
  145.1 12.2 %collective-permute-start.32 = (bf16[4,32,2048]{2,1,0:T(8,128)(2,1)S(1)}, bf16[4,32,2048]{2,1,0:T(8,128)(2,1)S(1)}, u32[]{:S(2)}, u32[]{:S(2)}) collective-permute-start(bf16[4,32,2048]{2,1,0:T(8,128)(2,1)S(1)} %collective-permute-done.24.refs_30_), channel_id=1, source_target_pairs={{0,1},{1,0},{2,3},{3,2},{4,5},{5,4},{6,7},{7,6},{8,9},{9,8},{10,11... | collective-permute-start | bytes 1572872 | tf_op jit(solution)/shard_map/ppermute | solution.py:17
  145.1 12.1 %collective-permute-start.31 = (bf16[4,32,2048]{2,1,0:T(8,128)(2,1)S(1)}, bf16[4,32,2048]{2,1,0:T(8,128)(2,1)S(1)}, u32[]{:S(2)}, u32[]{:S(2)}) collective-permute-start(bf16[4,32,2048]{2,1,0:T(8,128)(2,1)S(1)} %collective-permute-done.23.refs_29_), channel_id=1, source_target_pairs={{0,1},{1,0},{2,3},{3,2},{4,5},{5,4},{6,7},{7,6},{8,9},{9,8},{10,11... | collective-permute-start | bytes 1572872 | tf_op jit(solution)/shard_map/ppermute | solution.py:17
  145.6 16.0 %collective-permute-start.27 = (bf16[4,32,2048]{2,1,0:T(8,128)(2,1)S(1)}, bf16[4,32,2048]{2,1,0:T(8,128)(2,1)S(1)}, u32[]{:S(2)}, u32[]{:S(2)}) collective-permute-start(bf16[4,32,2048]{2,1,0:T(8,128)(2,1)S(1)} %collective-permute-done.23.refs_29_), channel_id=1, source_target_pairs={{0,2},{2,4},{4,6},{6,0},{1,3},{3,5},{5,7},{7,1},{8,10},{10,12},{12... | collective-permute-start | bytes 1572872 | tf_op jit(solution)/shard_map/ppermute | solution.py:21
  145.7 26.3 %collective-permute-start.25 = (bf16[4,32,2048]{2,1,0:T(8,128)(2,1)S(1)}, bf16[4,32,2048]{2,1,0:T(8,128)(2,1)S(1)}, u32[]{:S(2)}, u32[]{:S(2)}) collective-permute-start(bf16[4,32,2048]{2,1,0:T(8,128)(2,1)S(1)} %collective-permute-done.22.refs_28_), channel_id=1, source_target_pairs={{0,2},{2,4},{4,6},{6,0},{1,3},{3,5},{5,7},{7,1},{8,10},{10,12},{12... | collective-permute-start | bytes 1572872 | tf_op jit(solution)/shard_map/ppermute | solution.py:21
  154.7 17.3 %collective-permute-start.28 = (bf16[4,32,2048]{2,1,0:T(8,128)(2,1)S(1)}, bf16[4,32,2048]{2,1,0:T(8,128)(2,1)S(1)}, u32[]{:S(2)}, u32[]{:S(2)}) collective-permute-start(bf16[4,32,2048]{2,1,0:T(8,128)(2,1)S(1)} %collective-permute-done.26.refs_32_), channel_id=1, source_target_pairs={{0,6},{2,0},{4,2},{6,4},{1,7},{3,1},{5,3},{7,5},{8,14},{10,8},{12,... | collective-permute-start | bytes 1572872 | tf_op jit(solution)/shard_map/ppermute | solution.py:21
  157.3 15.6 %collective-permute-start.30 = (bf16[4,32,2048]{2,1,0:T(8,128)(2,1)S(1)}, bf16[4,32,2048]{2,1,0:T(8,128)(2,1)S(1)}, u32[]{:S(2)}, u32[]{:S(2)}) collective-permute-start(bf16[4,32,2048]{2,1,0:T(8,128)(2,1)S(1)} %collective-permute-done.22.refs_28_), channel_id=1, source_target_pairs={{0,1},{1,0},{2,3},{3,2},{4,5},{5,4},{6,7},{7,6},{8,9},{9,8},{10,11... | collective-permute-start | bytes 1572872 | tf_op jit(solution)/shard_map/ppermute | solution.py:17
  157.3 15.6 %collective-permute-start.34 = (bf16[4,32,2048]{2,1,0:T(8,128)(2,1)S(1)}, bf16[4,32,2048]{2,1,0:T(8,128)(2,1)S(1)}, u32[]{:S(2)}, u32[]{:S(2)}) collective-permute-start(bf16[4,32,2048]{2,1,0:T(8,128)(2,1)S(1)} %collective-permute-done.26.refs_32_), channel_id=1, source_target_pairs={{0,1},{1,0},{2,3},{3,2},{4,5},{5,4},{6,7},{7,6},{8,9},{9,8},{10,11... | collective-permute-start | bytes 1572872 | tf_op jit(solution)/shard_map/ppermute | solution.py:17
  (44 other events, 693.8 us)
